TPU v7x, 512 devices: a whole 4x8x8 slice. The times are simulated.
512 devices in a mesh: seq: 64 (over y, x, core), doc: 8 (over z).
Axes of the slice: x: 4, y: 8, z: 8, core: 2. Of those that a mesh axis runs over, the one named last changes fastest.
Arguments:
- grad_out: bfloat16 [8, 16384, 1024], P('doc', 'seq'), may hold values from -6 to 6
- pre_act: bfloat16 [8, 16384, 1024], P('doc', 'seq'), may hold values from -8 to 8
- word_of: int32 [8, 16384], P('doc', 'seq'), may hold values from 0 to 4095, as said below
- word_owner: int32 [8, 4096], P('doc'), may hold values from 0 to 63, as said below
- w_proj: bfloat16 [1024, 4096], P('seq', 'doc'), may hold values from -0.1875 to 0.1875
Outputs:
- word_grad: bfloat16 [8, 4096, 4096], P('doc', 'seq')
Inputs may be any that keep to these rules, and one draw needn't show every extreme that they name: `word_of`: within a document the entries never fall, start at 0 and take every value up to 4095. The bytes of one device meet at most 127 different words, exactly that many on some device of every document; every device but the first begins inside the last word of the device before it. `word_owner`: the owner of word w depends only on w modulo 64, and different remainders have different owners, so every owner gets 64 words and at most 2 words met by one device share an owner.
All inputs are finite; a program needn't handle non-finite values.
Results may differ from a plain program's by a relative error of at most 0.0049.
Values may be sent and summed in bfloat16 or wider, within the bound.
No kernel may reach another device: no remote copies, remote signals or barrier semaphores. Data moves between devices by JAX's collectives and lax.ppermute only.
A program may use at most 64 MiB of HBM per device.

v0:
```python
import jax
import jax.numpy as jnp
from jax import lax
from jax.sharding import PartitionSpec as P

inv_root_two = 0.7071067811865476
inv_root_tau = 0.3989422804014327


def slope_of(pre):
    value = pre.astype(jnp.float32)
    return (
        0.5 * (1.0 + jax.scipy.special.erf(value * inv_root_two))
        + value * jnp.exp(-0.5 * value * value) * inv_root_tau
    )


def shards(grad_out, pre_act, word_of, word_owner, w_proj):
    n_seq = lax.axis_size("seq")
    g_pre = (grad_out[0].astype(jnp.float32) * slope_of(pre_act[0])).astype(jnp.bfloat16)
    w_cols = lax.all_gather(w_proj, "doc", axis=1, tiled=True)
    w_full = lax.all_gather(w_cols, "seq", axis=0, tiled=True)
    word_ids = word_of[0]
    owner_row = word_owner[0]
    total_words = owner_row.shape[0]
    per_owner = total_words // n_seq
    slot_cap = 2 * (per_owner // n_seq)
    local_cap = slot_cap * n_seq
    first_word = word_ids[0]
    local_index = word_ids - first_word
    offsets = jnp.arange(local_cap, dtype=jnp.int32)
    global_ids = first_word + offsets
    present = global_ids <= word_ids[-1]
    owners = jnp.take(owner_row, jnp.minimum(global_ids, total_words - 1))
    target = jnp.where(present, owners * slot_cap + offsets // n_seq, local_cap)
    matches = target[None, :] == offsets[:, None]
    source = jnp.argmax(matches, axis=1)
    filled = jnp.any(matches, axis=1)
    slot_rows = jnp.where(filled, jnp.take(global_ids, source) // n_seq, per_owner)
    slot_rows = slot_rows.astype(jnp.float32).reshape(n_seq, slot_cap)
    byte_words = local_index[None, :] == offsets[:, None]
    projected = jnp.dot(g_pre, w_full, preferred_element_type=jnp.float32)
    partial_value = jnp.dot(
        byte_words.astype(jnp.float32),
        projected,
        precision=lax.Precision.HIGHEST,
        preferred_element_type=jnp.float32,
    )
    picked = jnp.take(partial_value, source, axis=0)
    received = lax.all_to_all(
        jnp.where(filled[:, None], picked, 0.0).reshape(n_seq, slot_cap, partial_value.shape[1]),
        "seq",
        split_axis=0,
        concat_axis=0,
        tiled=True,
    )
    row_ids = lax.all_to_all(slot_rows, "seq", split_axis=0, concat_axis=0, tiled=True)
    flat = received.reshape(local_cap, received.shape[2])
    owned_rows = jnp.arange(per_owner, dtype=jnp.int32)
    picker = (row_ids.reshape(-1).astype(jnp.int32)[None, :] == owned_rows[:, None]).astype(
        jnp.float32
    )
    summed = jnp.dot(
        picker, flat, precision=lax.Precision.HIGHEST, preferred_element_type=jnp.float32
    )
    return summed.astype(jnp.bfloat16)[None]


def solution(mesh):
    return jax.shard_map(
        shards,
        mesh=mesh,
        in_specs=(
            P("doc", "seq", None),
            P("doc", "seq", None),
            P("doc", "seq"),
            P("doc", None),
            P("seq", "doc"),
        ),
        out_specs=P("doc", "seq", None),
        check_vma=False,
    )
```

profile of v0, /device:TPU:1, one launch (start us, length us, event | category | flops | bytes accessed | tf_op | source)
XLA Modules:
  0.0 212.7 jit_solution(5644446789660786289)
XLA Ops:
  6.5 0.0 copy-start
  6.5 0.0 all-gather.2.cloned.1.call-start
  6.5 27.7 %all_gather.6 = bf16[16,4096]{1,0:T(8,128)(2,1)} all-gather(bf16[16,512]{1,0:T(8,128)(2,1)} %param.9), channel_id=1, replica_groups=mesh['seq'=64,'doc'=8] {'doc'}, dimensions={1}, use_global_device_ids=true | all-gather | bytes 147456 | tf_op jit(solution)/shard_map/all_gather | solution.py:21
  34.3 0.0 all-gather.2.cloned.1.call-update
  34.3 1.3 fusion.29
  35.5 0.7 fusion.23
  36.2 0.0 copy-done
  36.2 1.1 gather_fusion
  37.4 1.3 compare_select_fusion.3
  38.7 0.1 fusion.20
  38.8 0.2 reduce_or.12
  39.0 0.1 copy.12
  39.1 0.7 iota_reduce_fusion
  39.8 1.2 gather_fusion.1
  41.0 0.1 select_n.108
  41.1 0.1 copy.8
  41.2 0.7 copy.13
  42.0 17.2 %all-to-all-start = ((f32[64,1,2]{2,1,0:T(1,128)}), f32[64,1,2]{2,1,0:T(1,128)S(1)}, u32[]{:S(2)}, u32[]{:S(2)}) async-start(f32[64,1,2]{2,1,0:T(1,128)} %copy.13), calls=%async_computation | async-start | bytes 65536 | tf_op jit(solution)/shard_map/all_to_all | solution.py:57
  59.2 0.1 broadcast_in_dim.56
  59.3 0.2 broadcast_in_dim.58
  59.5 1.4 broadcast_subtract_fusion
  60.8 66.8 %all-gather.2.cloned.1.call-done = bf16[1024,4096]{1,0:T(8,128)(2,1)} async-done(((bf16[16,4096]{1,0:T(8,128)(2,1)}), bf16[1024,4096]{1,0:T(8,128)(2,1)}) %all-gather.2.cloned.1.call-update) | async-done | bytes 8388624 | tf_op jit(solution)/shard_map/all_gather | solution.py:22
  127.7 6.3 %fusion.9 = f32[256,4096]{1,0:T(8,128)S(1)} fusion(bf16[1024,4096]{1,0:T(8,128)(2,1)} %all-gather.2.cloned.1.call-done, bf16[1,256,1024]{2,1,0:T(8,128)(2,1)} %param.5, bf16[1,256,1024]{2,1,0:T(8,128)(2,1)} %param.6), kind=kOutput, calls=%fused_computation.18 | convolution fusion | flops 2150629376 | bytes 13631488 | tf_op jit(solution)/shard_map/dot_general | solution.py:42
  134.0 1.7 fusion.18
  135.8 2.6 %gather_fusion.2 = f32[128,4096]{1,0:T(8,128)} fusion(f32[128,4096]{1,0:T(8,128)S(1)} %fusion.18, s32[1024]{0:T(1024)S(1)} %pad_clamp_fusion), kind=kCustom, calls=%fused_computation.2 | custom fusion | bytes 4194816 | tf_op jit(solution)/shard_map/jit(_take)/gather | solution.py:49
  138.3 2.5 %gather.17 = f32[64,2,4096]{2,1,0:T(2,128)S(1)} reshape(f32[128,4096]{1,0:T(8,128)} %gather_fusion.2) | data formatting | bytes 4194304 | tf_op jit(solution)/shard_map/jit(_take)/gather | solution.py:49
  140.8 3.7 %select_select_fusion = f32[64,2,4096]{2,1,0:T(2,128)} fusion(f32[64,2,4096]{2,1,0:T(2,128)S(1)} %gather.17, pred[64,2]{1,0:T(8,128)(4,1)S(1)} %broadcast_in_dim.58, pred[64,2]{1,0:T(8,128)(4,1)S(1)} %broadcast_in_dim.56), kind=kLoop, calls=%fused_computation.5 | loop fusion | flops 1048576 | bytes 4194560 | tf_op jit(solution)/shard_map/jit(_where)/select_n | solution.py:51
  144.5 0.0 all-to-all-done
  144.6 5.9 %all-to-all-start.1 = ((f32[64,2,4096]{2,1,0:T(2,128)}), f32[64,2,4096]{2,1,0:T(2,128)S(1)}, u32[]{:S(2)}, u32[]{:S(2)}) async-start(f32[64,2,4096]{2,1,0:T(2,128)} %select_select_fusion), calls=%async_computation.1 | async-start | bytes 4194304 | tf_op jit(solution)/shard_map/all_to_all | solution.py:50
  150.4 0.1 convert_reduce_fusion
  150.5 0.1 convert_element_type.43
  150.7 49.5 %all-to-all-done.1 = f32[64,2,4096]{2,1,0:T(2,128)S(1)} async-done(((f32[64,2,4096]{2,1,0:T(2,128)}), f32[64,2,4096]{2,1,0:T(2,128)S(1)}, u32[]{:S(2)}, u32[]{:S(2)}) %all-to-all-start.1) | async-done | bytes 2097184 | tf_op jit(solution)/shard_map/all_to_all | solution.py:50
  200.1 2.5 %reshape.174 = f32[128,4096]{1,0:T(8,128)} reshape(f32[64,2,4096]{2,1,0:T(2,128)S(1)} %all-to-all-done.1) | data formatting | bytes 4194304 | tf_op jit(solution)/shard_map/reshape | solution.py:58
  202.6 3.3 %fusion = bf16[1,64,4096]{2,1,0:T(8,128)(2,1)} fusion(f32[128,4096]{1,0:T(8,128)} %reshape.174, s32[128]{0:T(128)S(1)} %convert_element_type.43), kind=kOutput, calls=%fused_computation.4 | convolution fusion | flops 402923520 | bytes 2621952 | tf_op jit(solution)/shard_map/dot_general | solution.py:63
  (5 shorter events, 0.0 us)
Async XLA Ops:
  6.5 29.7 %copy-start = (s32[1,4096]{1,0:T(1,128)S(1)}, s32[1,4096]{1,0:T(1,128)}, u32[]{:S(2)}) copy-start(s32[1,4096]{1,0:T(1,128)} %param.8) | copy-start | bytes 49156
  6.5 121.1 %all-gather.2.cloned.1.call-start = ((), (), s32[]{:S(2)}) async-start(), calls=%async_computation.2 | async-start | bytes 8519680 | tf_op jit(solution)/shard_map/all_gather | solution.py:22
  42.0 102.6 %all-to-all-start = ((f32[64,1,2]{2,1,0:T(1,128)}), f32[64,1,2]{2,1,0:T(1,128)S(1)}, u32[]{:S(2)}, u32[]{:S(2)}) async-start(f32[64,1,2]{2,1,0:T(1,128)} %copy.13), calls=%async_computation | async-start | bytes 65536 | tf_op jit(solution)/shard_map/all_to_all | solution.py:57
  144.6 55.6 %all-to-all-start.1 = ((f32[64,2,4096]{2,1,0:T(2,128)}), f32[64,2,4096]{2,1,0:T(2,128)S(1)}, u32[]{:S(2)}, u32[]{:S(2)}) async-start(f32[64,2,4096]{2,1,0:T(2,128)} %select_select_fusion), calls=%async_computation.1 | async-start | bytes 4194304 | tf_op jit(solution)/shard_map/all_to_all | solution.py:50
Sparse Core Ops, SparseCore 0:
  34.4 93.2 all-gather.1
where the time goes:
time: 214 us; the launch traced here: 213 us
  waiting for transfers between devices  116 us (54%)
  blocking collectives  27.7 us (13%)
  starting transfers between devices  23.1 us (11%)
  between operations  13.5 us (6%)
  local copies, waits for them, and re-layouts  12.8 us (6%)
  matrix products  11.3 us (5%)
  other arithmetic  7.99 us (4%)
    all_gather x1, waiting for transfers between devices, shards(): w_full = lax.all_gather(w_cols, 'seq', axis=0, tiled=True)  66.8 us
    all_to_all x1, waiting for transfers between devices, shards(): lax.all_to_all(jnp.where(filled[:, None], picked, 0.0).reshape(n_seq, slo...  49.5 us
    all_gather x1, blocking collectives, shards(): w_cols = lax.all_gather(w_proj, 'doc', axis=1, tiled=True)  27.7 us
    all_to_all x1, starting transfers between devices, shards(): lax.all_to_all(slot_rows, 'seq', split_axis=0, concat_axis=0, tiled=True)  17.2 us
    dot_general x1, matrix products, shards(): projected = jnp.dot(g_pre, w_full, preferred_element_type=jnp.float32)  6.32 us
    all_to_all x1, starting transfers between devices, shards(): lax.all_to_all(jnp.where(filled[:, None], picked, 0.0).reshape(n_seq, slo...  5.87 us
    gather x2, local copies, waits for them, and re-layouts, shards(): picked = jnp.take(partial_value, source, axis=0)  5.06 us
  transfers between devices with their start and end apart: 3, of which 2 were waited for; matrix products, arithmetic and copies ran while one was open for 12% of the time, Pallas kernels for 0%

commit v1 on v0

v1 whole, which is shorter than its diff:
```python
import jax
import jax.numpy as jnp
from jax import lax
from jax.experimental import pallas as pl
from jax.experimental.pallas import tpu as pltpu
from jax.sharding import PartitionSpec as P

inv_root_two = 0.7071067811865476
inv_root_tau = 0.3989422804014327
BF16 = jnp.bfloat16
F32 = jnp.float32
LANES = 128


def slope_of(value):
    return (
        0.5 * (1.0 + lax.erf(value * inv_root_two))
        + value * jnp.exp(-0.5 * value * value) * inv_root_tau
    )


def word_sums_kernel(n_seq, word_ref, owner_ref, grad_ref, pre_ref, w_ref, out_ref):
    slots = 2 * n_seq
    width = grad_ref.shape[1]
    words = word_ref[...]
    rank = words // n_seq
    row = lax.broadcasted_iota(jnp.int32, (slots, LANES), 0)
    lane = lax.broadcasted_iota(jnp.int32, (slots, LANES), 1)
    owned = (owner_ref[...] == row // 2) & (lane < n_seq)
    remainder = jnp.sum(jnp.where(owned, lane, 0).astype(F32), axis=1, keepdims=True)
    parity = lax.broadcasted_iota(jnp.int32, (slots, 1), 0) % 2
    match = (words % n_seq == remainder.astype(jnp.int32)) & (rank % 2 == parity)
    ids = jnp.max(jnp.where(match, rank, 0).astype(F32), axis=1, keepdims=True)
    picks = jnp.where(match, 1.0, 0.0).astype(BF16)
    step = 256
    for at in range(0, width, step):
        cols = slice(at, at + step)
        g_pre = (grad_ref[:, cols].astype(F32) * slope_of(pre_ref[:, cols].astype(F32))).astype(BF16)
        out_ref[:, cols] = jnp.dot(picks, g_pre, preferred_element_type=F32).astype(BF16)
    out_ref[:, width : width + LANES] = jnp.broadcast_to(ids, (slots, LANES)).astype(BF16)
    depth = w_ref.shape[0]
    for at in range(0, slots, depth):
        out_ref[at : at + depth, width + LANES :] = w_ref[...]


def own_rows_kernel(per_owner, width, got_ref, out_ref):
    slots = got_ref.shape[0]
    ids = jnp.transpose(got_ref[:, width : width + LANES].astype(F32))[0:1, :]
    rows = lax.broadcasted_iota(jnp.int32, (per_owner, slots), 0)
    picks = jnp.where(rows == ids.astype(jnp.int32), 1.0, 0.0).astype(BF16)
    source = lax.broadcasted_iota(jnp.int32, (LANES, LANES), 0)
    target = lax.broadcasted_iota(jnp.int32, (LANES, LANES), 1)
    moved = (source // 2 % 8) * 16 + (source // 16) * 2 + source % 2
    order = jnp.where(moved == target, 1.0, 0.0).astype(BF16)
    for at in range(0, width, LANES):
        cols = slice(at, at + LANES)
        summed = jnp.dot(picks, got_ref[:, cols], preferred_element_type=F32).astype(BF16)
        summed = jnp.dot(summed, order, preferred_element_type=F32).astype(BF16)
        for copy in range(out_ref.shape[0]):
            out_ref[copy, :, cols] = summed


def project_kernel(masks, rows_ref, *refs):
    pieces, out_ref, w_ref = refs[:-2], refs[-2], refs[-1]
    inner = len(masks)
    depth = LANES // inner
    outer = w_ref.shape[0] // LANES
    here = lax.axis_index("seq") % inner
    each = inner // len(pieces)
    for slot, mask in enumerate(masks):
        source = pieces[slot // each]
        place = (here ^ mask) * depth
        for tile in range(outer):
            start = pl.multiple_of(tile * LANES + place, depth)
            at = (slot % each) * LANES + tile * depth
            w_ref[pl.ds(start, depth), :] = source[at : at + depth, :]
    out_ref[...] = jnp.dot(rows_ref[...], w_ref[...], preferred_element_type=F32).astype(BF16)


def lay_out_kernel(back_ref, out_ref):
    cols = back_ref.shape[2]
    for block in range(back_ref.shape[0]):
        out_ref[:, block * cols : (block + 1) * cols] = back_ref[block]


def shards(grad_out, pre_act, word_of, word_owner, w_proj):
    n_seq = lax.axis_size("seq")
    n_doc = lax.axis_size("doc")
    width = grad_out.shape[2]
    slots = 2 * n_seq
    per_owner = word_owner.shape[1] // n_seq
    depth, cols = w_proj.shape
    total = width + LANES + cols
    params = pltpu.CompilerParams(vmem_limit_bytes=VMEM_LIMIT)

    sums = pl.pallas_call(
        lambda *refs: word_sums_kernel(n_seq, *refs),
        out_shape=jax.ShapeDtypeStruct((slots, total), BF16),
        grid=(1,),
        in_specs=[
            pl.BlockSpec(word_of.shape, lambda i: (0, 0)),
            pl.BlockSpec((1, LANES), lambda i: (0, 0)),
            pl.BlockSpec(grad_out.shape[1:], lambda i: (0, 0)),
            pl.BlockSpec(pre_act.shape[1:], lambda i: (0, 0)),
            pl.BlockSpec(w_proj.shape, lambda i: (0, 0)),
        ],
        out_specs=pl.BlockSpec((slots, total), lambda i: (0, 0)),
        compiler_params=params,
        cost_estimate=pl.CostEstimate(flops=20_000_000, bytes_accessed=3_000_000, transcendentals=500_000),
        name="word_sums",
    )(word_of, word_owner, grad_out[0], pre_act[0], w_proj)
    got = lax.all_to_all(
        sums.reshape(n_seq, 2, total), "seq", 0, 0, tiled=True
    ).reshape(slots, total)

    rows = pl.pallas_call(
        lambda *refs: own_rows_kernel(per_owner, width, *refs),
        out_shape=jax.ShapeDtypeStruct((n_doc, per_owner, width), BF16),
        compiler_params=params,
        cost_estimate=pl.CostEstimate(flops=20_000_000, bytes_accessed=1_500_000, transcendentals=0),
        name="own_rows",
    )(got)
    rows = lax.all_to_all(rows, "doc", 0, 0, tiled=True).reshape(n_doc * per_owner, width)

    have = got[:, width + LANES :]
    masks = [0]
    for bit in BITS[:-1]:
        other = lax.ppermute(have, "seq", [(i, i ^ bit) for i in range(n_seq)])
        have = jnp.concatenate([have, other], axis=0)
        masks += [mask ^ bit for mask in masks]
    other = lax.ppermute(have, "seq", [(i, i ^ BITS[-1]) for i in range(n_seq)])
    masks += [mask ^ BITS[-1] for mask in masks]

    part = pl.pallas_call(
        lambda *refs: project_kernel(masks, *refs),
        out_shape=jax.ShapeDtypeStruct((n_doc * per_owner, cols), BF16),
        scratch_shapes=[pltpu.VMEM((width, cols), BF16)],
        compiler_params=params,
        cost_estimate=pl.CostEstimate(flops=600_000_000, bytes_accessed=2_500_000, transcendentals=0),
        name="project",
    )(rows, have, other)
    back = lax.all_to_all(part.reshape(n_doc, per_owner, cols), "doc", 0, 0, tiled=True)
    out = pl.pallas_call(
        lay_out_kernel,
        out_shape=jax.ShapeDtypeStruct((per_owner, n_doc * cols), BF16),
        compiler_params=params,
        name="lay_out",
    )(back)
    return out[None]


BITS = (4, 2, 1)
VMEM_LIMIT = 16 * 1024 * 1024


def solution(mesh):
    return jax.shard_map(
        shards,
        mesh=mesh,
        in_specs=(
            P("doc", "seq", None),
            P("doc", "seq", None),
            P("doc", "seq"),
            P("doc", None),
            P("seq", "doc"),
        ),
        out_specs=P("doc", "seq", None),
        check_vma=False,
    )
```

time: 214 us -> 95.5 us (0.45)
  waiting for transfers between devices: 116 us -> 18.1 us
  blocking collectives: 27.7 us -> 47.3 us
  between operations: 13.5 us -> 0.07 us
  matrix products: 11.3 us -> 0 us
  local copies, waits for them, and re-layouts: 12.8 us -> 4.52 us
  other arithmetic: 7.99 us -> 0.05 us
  Pallas kernels: 0 us -> 3.83 us
    all_gather x1 -> x0, waiting for transfers between devices: 66.8 us -> none  [shards(): w_full = lax.all_gather(w_cols, 'seq', axis=0, tiled=True)]
    all_to_all x0 -> x2, blocking collectives: none -> 47.3 us  [the longest x1 27.1 us: shards(): lax.all_to_all(sums.reshape(n_seq, 2, total), 'seq', 0, 0, tiled=True)]
    all_to_all x2 -> x1, waiting for transfers between devices: 49.5 us -> 7.27 us  [shards(): lax.all_to_all(rows, 'doc', 0, 0, tiled=True)]
    all_gather x1 -> x0, blocking collectives: 27.7 us -> none  [shards(): w_cols = lax.all_gather(w_proj, 'doc', axis=1, tiled=True)]
    all_to_all x2 -> x1, starting transfers between devices: 23.1 us -> 10 us  [shards(): lax.all_to_all(rows, 'doc', 0, 0, tiled=True)]
    dot_general x3 -> x0, matrix products: 11.3 us -> none  [the longest x1 6.32 us: shards(): projected = jnp.dot(g_pre, w_full, preferred_element_type=jnp.float32)]
    ppermute x0 -> x3, starting transfers between devices: none -> 11 us  [the longest x2 6.8 us: shards(): other = lax.ppermute(have, 'seq', [(i, i ^ bit) for i in range(n_seq)])]
    ppermute x0 -> x3, waiting for transfers between devices: none -> 10.8 us  [the longest x2 9.32 us: shards(): other = lax.ppermute(have, 'seq', [(i, i ^ bit) for i in range(n_seq)])]
  transfers between devices with their start and end apart: 3 -> 4, of which waited for: 2 -> 4; matrix products, arithmetic and copies ran while one was open for 12% -> 0% of each run, Pallas kernels for 0% -> 0%
where the time goes in v1:
time: 95.5 us; the launch traced here: 95 us
  blocking collectives  47.3 us (50%)
  starting transfers between devices  21.1 us (22%)
  waiting for transfers between devices  18.1 us (19%)
  local copies, waits for them, and re-layouts  4.52 us (5%)
  Pallas kernels  3.83 us (4%)
    all_to_all x1, blocking collectives, shards(): lax.all_to_all(sums.reshape(n_seq, 2, total), 'seq', 0, 0, tiled=True)  27.1 us
    all_to_all x1, blocking collectives, shards(): lax.all_to_all(part.reshape(n_doc, per_owner, cols), 'doc', 0, 0, tiled=T...  20.2 us
    all_to_all x1, starting transfers between devices, shards(): lax.all_to_all(rows, 'doc', 0, 0, tiled=True)  10 us
    ppermute x2, waiting for transfers between devices, shards(): other = lax.ppermute(have, 'seq', [(i, i ^ bit) for i in range(n_seq)])  9.32 us
    all_to_all x1, waiting for transfers between devices, shards(): lax.all_to_all(rows, 'doc', 0, 0, tiled=True)  7.27 us
    ppermute x2, starting transfers between devices, shards(): other = lax.ppermute(have, 'seq', [(i, i ^ bit) for i in range(n_seq)])  6.8 us
    ppermute x1, starting transfers between devices, shards(): other = lax.ppermute(have, 'seq', [(i, i ^ BITS[-1]) for i in range(n_seq)])  4.23 us
    unnamed x10, local copies, waits for them, and re-layouts  4.19 us
  transfers between devices with their start and end apart: 4, of which 4 were waited for; matrix products, arithmetic and copies ran while one was open for 0% of the time, Pallas kernels for 0%

profile of v1, /device:TPU:1, one launch (start us, length us, event | category | flops | bytes accessed | tf_op | source)
XLA Modules:
  0.0 95.0 jit_solution(17475800198306492476)
XLA Ops:
  0.0 0.0 copy-start.4
  0.0 0.7 copy-done.4
  0.7 0.0 copy-start
  0.7 1.0 %copy-done = bf16[1,256,1024]{2,1,0:T(8,128)(2,1)S(1)} copy-done((bf16[1,256,1024]{2,1,0:T(8,128)(2,1)S(1)}, bf16[1,256,1024]{2,1,0:T(8,128)(2,1)}, u32[]{:S(2)}) %copy-start) | copy-done | bytes 524312
  1.7 0.0 copy-start.1
  1.7 1.0 %copy-done.1 = bf16[1,256,1024]{2,1,0:T(8,128)(2,1)S(1)} copy-done((bf16[1,256,1024]{2,1,0:T(8,128)(2,1)S(1)}, bf16[1,256,1024]{2,1,0:T(8,128)(2,1)}, u32[]{:S(2)}) %copy-start.1) | copy-done | bytes 524312
  2.8 0.0 copy-start.2
  2.8 0.7 copy-done.2
  3.5 0.0 copy-start.3
  3.5 0.7 copy-done.3
  4.2 0.7 word_sums.1
  4.9 0.2 reshape.12
  5.1 27.1 %all_to_all.15 = bf16[64,2,1664]{2,1,0:T(2,128)(2,1)S(1)} all-to-all(bf16[64,2,1664]{2,1,0:T(2,128)(2,1)S(1)} %reshape.12), channel_id=1, replica_groups=mesh['seq'=64,'doc'=8] {'seq'}, dimensions={0} | all-to-all | bytes 851968 | tf_op jit(solution)/shard_map/all_to_all | solution.py:112
  32.2 0.2 reshape.13.refs_0_
  32.3 1.5 %own_rows.1 = bf16[8,64,1024]{2,1,0:T(8,128)(2,1)} custom-call(bf16[128,1664]{1,0:T(8,128)(2,1)S(1)} %reshape.13.refs_0_), custom_call_target="tpu_custom_call" | custom-call | flops 20000000 | bytes 1500000 | tf_op jit(solution)/shard_map/own_rows/pallas_call | solution.py:116
  33.9 10.0 %all-to-all-start.1 = ((bf16[8,64,1024]{2,1,0:T(8,128)(2,1)}), bf16[8,64,1024]{2,1,0:T(8,128)(2,1)S(1)}, u32[]{:S(2)}, u32[]{:S(2)}) async-start(bf16[8,64,1024]{2,1,0:T(8,128)(2,1)} %own_rows.1), calls=%async_computation.1 | async-start | bytes 2097152 | tf_op jit(solution)/shard_map/all_to_all | solution.py:123
  43.9 3.8 %collective-permute-start = (bf16[128,512]{1,0:T(8,128)(2,1)S(1)}, bf16[128,512]{1,0:T(8,128)(2,1)S(1)}, u32[]{:S(2)}, u32[]{:S(2)}) collective-permute-start(bf16[128,512]{1,0:T(8,128)(2,1)S(1)} %slice.4), channel_id=1, source_target_pairs={{0,32},{8,40},{16,48},{24,56},{32,0},{40,8},{48,16},{56,24},{64,96... | collective-permute-start | bytes 393224 | tf_op jit(solution)/shard_map/ppermute | solution.py:128
  47.7 4.0 %collective-permute-done = bf16[128,512]{1,0:T(8,128)(2,1)S(1)} collective-permute-done((bf16[128,512]{1,0:T(8,128)(2,1)S(1)}, bf16[128,512]{1,0:T(8,128)(2,1)S(1)}, u32[]{:S(2)}, u32[]{:S(2)}) %collective-permute-start) | collective-permute-done | bytes 131104 | tf_op jit(solution)/shard_map/ppermute | solution.py:128
  51.8 3.0 %collective-permute-start.1 = (bf16[256,512]{1,0:T(8,128)(2,1)S(1)}, bf16[256,512]{1,0:T(8,128)(2,1)S(1)}, u32[]{:S(2)}, u32[]{:S(2)}) collective-permute-start(bf16[256,512]{1,0:T(8,128)(2,1)S(1)} %pad_maximum_fusion.1), channel_id=1, source_target_pairs={{0,16},{8,24},{16,0},{24,8},{32,48},{40,56},{48,32},{56,40},{64,80... | collective-permute-start | bytes 786440 | tf_op jit(solution)/shard_map/ppermute | solution.py:128
  54.8 5.3 %collective-permute-done.1 = bf16[256,512]{1,0:T(8,128)(2,1)S(1)} collective-permute-done((bf16[256,512]{1,0:T(8,128)(2,1)S(1)}, bf16[256,512]{1,0:T(8,128)(2,1)S(1)}, u32[]{:S(2)}, u32[]{:S(2)}) %collective-permute-start.1) | collective-permute-done | bytes 262176 | tf_op jit(solution)/shard_map/ppermute | solution.py:128
  60.1 4.2 %collective-permute-start.2 = (bf16[512,512]{1,0:T(8,128)(2,1)S(1)}, bf16[512,512]{1,0:T(8,128)(2,1)S(1)}, u32[]{:S(2)}, u32[]{:S(2)}) collective-permute-start(bf16[512,512]{1,0:T(8,128)(2,1)S(1)} %pad_maximum_fusion.refs_1_), channel_id=1, source_target_pairs={{0,8},{8,0},{16,24},{24,16},{32,40},{40,32},{48,56},{56,48},{64,72... | collective-permute-start | bytes 1572872 | tf_op jit(solution)/shard_map/ppermute | solution.py:131
  64.4 1.5 %collective-permute-done.2.refs_2_ = bf16[512,512]{1,0:T(8,128)(2,1)S(1)} collective-permute-done((bf16[512,512]{1,0:T(8,128)(2,1)S(1)}, bf16[512,512]{1,0:T(8,128)(2,1)S(1)}, u32[]{:S(2)}, u32[]{:S(2)}) %collective-permute-start.2) | collective-permute-done | bytes 524320 | tf_op jit(solution)/shard_map/ppermute | solution.py:131
  65.9 7.3 %all-to-all-done.1 = bf16[8,64,1024]{2,1,0:T(8,128)(2,1)S(1)} async-done(((bf16[8,64,1024]{2,1,0:T(8,128)(2,1)}), bf16[8,64,1024]{2,1,0:T(8,128)(2,1)S(1)}, u32[]{:S(2)}, u32[]{:S(2)}) %all-to-all-start.1) | async-done | bytes 1048608 | tf_op jit(solution)/shard_map/all_to_all | solution.py:123
  73.1 0.8 project.1
  73.9 20.2 %all_to_all.16.back_ref = bf16[8,64,512]{2,1,0:T(8,128)(2,1)S(1)} all-to-all(bf16[8,64,512]{2,1,0:T(8,128)(2,1)S(1)} %bitcast.6), channel_id=1, replica_groups=mesh['seq'=64,'doc'=8] {'doc'}, dimensions={0} | all-to-all | bytes 1048576 | tf_op jit(solution)/shard_map/all_to_all | solution.py:142
  94.2 0.8 lay_out.1
  (3 shorter events, 0.1 us)
Async XLA Ops:
  0.0 0.7 copy-start.4
  0.7 1.0 %copy-start = (bf16[1,256,1024]{2,1,0:T(8,128)(2,1)S(1)}, bf16[1,256,1024]{2,1,0:T(8,128)(2,1)}, u32[]{:S(2)}) copy-start(bf16[1,256,1024]{2,1,0:T(8,128)(2,1)} %param.5) | copy-start | bytes 1572868
  1.7 1.0 %copy-start.1 = (bf16[1,256,1024]{2,1,0:T(8,128)(2,1)S(1)}, bf16[1,256,1024]{2,1,0:T(8,128)(2,1)}, u32[]{:S(2)}) copy-start(bf16[1,256,1024]{2,1,0:T(8,128)(2,1)} %param.6) | copy-start | bytes 1572868
  2.8 0.7 copy-start.2
  3.5 0.7 copy-start.3
  33.9 39.3 %all-to-all-start.1 = ((bf16[8,64,1024]{2,1,0:T(8,128)(2,1)}), bf16[8,64,1024]{2,1,0:T(8,128)(2,1)S(1)}, u32[]{:S(2)}, u32[]{:S(2)}) async-start(bf16[8,64,1024]{2,1,0:T(8,128)(2,1)} %own_rows.1), calls=%async_computation.1 | async-start | bytes 2097152 | tf_op jit(solution)/shard_map/all_to_all | solution.py:123
  43.9 7.8 %collective-permute-start = (bf16[128,512]{1,0:T(8,128)(2,1)S(1)}, bf16[128,512]{1,0:T(8,128)(2,1)S(1)}, u32[]{:S(2)}, u32[]{:S(2)}) collective-permute-start(bf16[128,512]{1,0:T(8,128)(2,1)S(1)} %slice.4), channel_id=1, source_target_pairs={{0,32},{8,40},{16,48},{24,56},{32,0},{40,8},{48,16},{56,24},{64,96... | collective-permute-start | bytes 393224 | tf_op jit(solution)/shard_map/ppermute | solution.py:128
  51.8 8.3 %collective-permute-start.1 = (bf16[256,512]{1,0:T(8,128)(2,1)S(1)}, bf16[256,512]{1,0:T(8,128)(2,1)S(1)}, u32[]{:S(2)}, u32[]{:S(2)}) collective-permute-start(bf16[256,512]{1,0:T(8,128)(2,1)S(1)} %pad_maximum_fusion.1), channel_id=1, source_target_pairs={{0,16},{8,24},{16,0},{24,8},{32,48},{40,56},{48,32},{56,40},{64,80... | collective-permute-start | bytes 786440 | tf_op jit(solution)/shard_map/ppermute | solution.py:128
  60.1 5.8 %collective-permute-start.2 = (bf16[512,512]{1,0:T(8,128)(2,1)S(1)}, bf16[512,512]{1,0:T(8,128)(2,1)S(1)}, u32[]{:S(2)}, u32[]{:S(2)}) collective-permute-start(bf16[512,512]{1,0:T(8,128)(2,1)S(1)} %pad_maximum_fusion.refs_1_), channel_id=1, source_target_pairs={{0,8},{8,0},{16,24},{24,16},{32,40},{40,32},{48,56},{56,48},{64,72... | collective-permute-start | bytes 1572872 | tf_op jit(solution)/shard_map/ppermute | solution.py:131

commit v2 on v1

--- a/solution.py
+++ b/solution.py
@@ -19,7 +19,7 @@
     )
 
 
-def word_sums_kernel(n_seq, word_ref, owner_ref, grad_ref, pre_ref, w_ref, out_ref):
+def word_sums_kernel(n_seq, word_ref, owner_ref, grad_ref, pre_ref, out_ref):
     slots = 2 * n_seq
     width = grad_ref.shape[1]
     words = word_ref[...]
@@ -38,9 +38,23 @@
         g_pre = (grad_ref[:, cols].astype(F32) * slope_of(pre_ref[:, cols].astype(F32))).astype(BF16)
         out_ref[:, cols] = jnp.dot(picks, g_pre, preferred_element_type=F32).astype(BF16)
     out_ref[:, width : width + LANES] = jnp.broadcast_to(ids, (slots, LANES)).astype(BF16)
-    depth = w_ref.shape[0]
-    for at in range(0, slots, depth):
-        out_ref[at : at + depth, width + LANES :] = w_ref[...]
+
+
+def pack_kernel(sums_ref, w_ref, out_ref):
+    slots, width = sums_ref.shape
+    blocks, depth, cols = w_ref.shape
+    out_ref[:, :width] = sums_ref[...]
+    out_row = lax.broadcasted_iota(jnp.int32, (slots, blocks * depth), 0)
+    w_row = lax.broadcasted_iota(jnp.int32, (slots, blocks * depth), 1)
+    block = out_row // 16 % 2 * 4 + out_row // 4 % 4
+    inner = out_row // 2 % 2 * 4 + out_row % 2
+    flat = w_ref[...].astype(F32).reshape(blocks * depth, cols).astype(BF16)
+    for h in range(2):
+        chosen = jnp.where(w_row == block * depth + inner + 2 * h, 1.0, 0.0).astype(BF16)
+        first = width + h * cols
+        out_ref[:, first : first + cols] = jnp.dot(
+            chosen, flat, preferred_element_type=F32
+        ).astype(BF16)
 
 
 def own_rows_kernel(per_owner, width, got_ref, out_ref):
@@ -62,18 +76,19 @@
 
 def project_kernel(masks, rows_ref, *refs):
     pieces, out_ref, w_ref = refs[:-2], refs[-2], refs[-1]
-    inner = len(masks)
-    depth = LANES // inner
-    outer = w_ref.shape[0] // LANES
-    here = lax.axis_index("seq") % inner
-    each = inner // len(pieces)
+    cols = w_ref.shape[1]
+    me = lax.axis_index("seq")
+    here = lax.axis_index("doc") % 2 * 2 + me % 2
+    each = len(masks) // len(pieces)
+    depth = LANES // (2 * len(masks))
     for slot, mask in enumerate(masks):
         source = pieces[slot // each]
-        place = (here ^ mask) * depth
-        for tile in range(outer):
-            start = pl.multiple_of(tile * LANES + place, depth)
-            at = (slot % each) * LANES + tile * depth
-            w_ref[pl.ds(start, depth), :] = source[at : at + depth, :]
+        place = (here ^ mask) * (2 * depth)
+        for h in range(2):
+            for tile in range(w_ref.shape[0] // LANES):
+                start = pl.multiple_of(tile * LANES + h * depth + place, depth)
+                at = (slot % each) * LANES + tile * depth
+                w_ref[pl.ds(start, depth), :] = source[at : at + depth, h * cols : (h + 1) * cols]
     out_ref[...] = jnp.dot(rows_ref[...], w_ref[...], preferred_element_type=F32).astype(BF16)
 
 
@@ -90,27 +105,45 @@
     slots = 2 * n_seq
     per_owner = word_owner.shape[1] // n_seq
     depth, cols = w_proj.shape
-    total = width + LANES + cols
+    total = width + LANES + 2 * cols
+    groups = [
+        [32 * y2 + 16 * y1 + 8 * y0 + 2 * x + c for y0 in range(2) for x in range(4)]
+        for y2 in range(2)
+        for y1 in range(2)
+        for c in range(2)
+    ]
+    w_docs = lax.all_to_all(
+        jnp.broadcast_to(
+            w_proj.reshape(1, 2, depth // 2, cols), (n_doc // 2, 2, depth // 2, cols)
+        ).reshape(n_doc, depth // 2, cols),
+        "doc", 0, 0, tiled=True,
+    )
     params = pltpu.CompilerParams(vmem_limit_bytes=VMEM_LIMIT)
 
     sums = pl.pallas_call(
         lambda *refs: word_sums_kernel(n_seq, *refs),
-        out_shape=jax.ShapeDtypeStruct((slots, total), BF16),
+        out_shape=jax.ShapeDtypeStruct((slots, width + LANES), BF16),
         grid=(1,),
         in_specs=[
             pl.BlockSpec(word_of.shape, lambda i: (0, 0)),
             pl.BlockSpec((1, LANES), lambda i: (0, 0)),
             pl.BlockSpec(grad_out.shape[1:], lambda i: (0, 0)),
             pl.BlockSpec(pre_act.shape[1:], lambda i: (0, 0)),
-            pl.BlockSpec(w_proj.shape, lambda i: (0, 0)),
         ],
-        out_specs=pl.BlockSpec((slots, total), lambda i: (0, 0)),
+        out_specs=pl.BlockSpec((slots, width + LANES), lambda i: (0, 0)),
         compiler_params=params,
         cost_estimate=pl.CostEstimate(flops=20_000_000, bytes_accessed=3_000_000, transcendentals=500_000),
         name="word_sums",
-    )(word_of, word_owner, grad_out[0], pre_act[0], w_proj)
+    )(word_of, word_owner, grad_out[0], pre_act[0])
+    packed = pl.pallas_call(
+        pack_kernel,
+        out_shape=jax.ShapeDtypeStruct((slots, total), BF16),
+        compiler_params=params,
+        cost_estimate=pl.CostEstimate(flops=20_000_000, bytes_accessed=1_000_000, transcendentals=0),
+        name="pack",
+    )(sums, w_docs)
     got = lax.all_to_all(
-        sums.reshape(n_seq, 2, total), "seq", 0, 0, tiled=True
+        packed.reshape(n_seq, 2, total), "seq", 0, 0, tiled=True
     ).reshape(slots, total)
 
     rows = pl.pallas_call(
@@ -120,16 +153,13 @@
         cost_estimate=pl.CostEstimate(flops=20_000_000, bytes_accessed=1_500_000, transcendentals=0),
         name="own_rows",
     )(got)
-    rows = lax.all_to_all(rows, "doc", 0, 0, tiled=True).reshape(n_doc * per_owner, width)
+    rows = lax.all_to_all(rows, "seq", 0, 0, tiled=True, axis_index_groups=groups).reshape(n_doc * per_owner, width)
 
     have = got[:, width + LANES :]
-    masks = [0]
-    for bit in BITS[:-1]:
-        other = lax.ppermute(have, "seq", [(i, i ^ bit) for i in range(n_seq)])
-        have = jnp.concatenate([have, other], axis=0)
-        masks += [mask ^ bit for mask in masks]
-    other = lax.ppermute(have, "seq", [(i, i ^ BITS[-1]) for i in range(n_seq)])
-    masks += [mask ^ BITS[-1] for mask in masks]
+    other = lax.ppermute(have, "doc", [(i, i ^ 1) for i in range(n_doc)])
+    have = jnp.concatenate([have, other], axis=0)
+    other = lax.ppermute(have, "seq", [(i, i ^ 1) for i in range(n_seq)])
+    masks = [0, 2, 1, 3]
 
     part = pl.pallas_call(
         lambda *refs: project_kernel(masks, *refs),
@@ -139,7 +169,7 @@
         cost_estimate=pl.CostEstimate(flops=600_000_000, bytes_accessed=2_500_000, transcendentals=0),
         name="project",
     )(rows, have, other)
-    back = lax.all_to_all(part.reshape(n_doc, per_owner, cols), "doc", 0, 0, tiled=True)
+    back = lax.all_to_all(part.reshape(n_doc, per_owner, cols), "seq", 0, 0, tiled=True, axis_index_groups=groups)
     out = pl.pallas_call(
         lay_out_kernel,
         out_shape=jax.ShapeDtypeStruct((per_owner, n_doc * cols), BF16),
@@ -149,7 +179,6 @@
     return out[None]
 
 
-BITS = (4, 2, 1)
 VMEM_LIMIT = 16 * 1024 * 1024
 
 

time: 95.5 us -> 86.3 us (0.904)
  waiting for transfers between devices: 18.1 us -> 13 us
  blocking collectives: 47.3 us -> 43.3 us
    ppermute x3 -> x2, starting transfers between devices: 11 us -> 5.6 us  [the longest x1 3.41 us: shards(): other = lax.ppermute(have, 'seq', [(i, i ^ 1) for i in range(n_seq)])]
    all_to_all x1 -> x2, starting transfers between devices: 10 us -> 15.1 us  [the longest x1 11 us: shards(): lax.all_to_all(jnp.broadcast_to(w_proj.reshape(1, 2, depth // 2, cols), (...]
    all_to_all x2, blocking collectives: 47.3 us -> 43.3 us  [the longest x1 30.4 us: shards(): lax.all_to_all(packed.reshape(n_seq, 2, total), 'seq', 0, 0, tiled=True)]
    all_to_all x1 -> x2, waiting for transfers between devices: 7.27 us -> 4.62 us  [the longest x1 3.76 us: shards(): lax.all_to_all(jnp.broadcast_to(w_proj.reshape(1, 2, depth // 2, cols), (...]
    ppermute x3 -> x2, waiting for transfers between devices: 10.8 us -> 8.43 us  [the longest x1 6.91 us: shards(): other = lax.ppermute(have, 'doc', [(i, i ^ 1) for i in range(n_doc)])]
    unnamed x10 -> x8, local copies, waits for them, and re-layouts: 4.19 us -> 2.75 us
    broadcast_in_dim x0 -> x1, local copies, waits for them, and re-layouts: none -> 1.35 us  [shards(): jnp.broadcast_to(w_proj.reshape(1, 2, depth // 2, cols), (n_doc // 2, 2,...]
  transfers between devices with their start and end apart: 4 -> 4, of which waited for: 4 -> 4; matrix products, arithmetic and copies ran while one was open for 0% -> 0% of each run, Pallas kernels for 0% -> 1%
where the time goes in v2:
time: 86.3 us; the launch traced here: 85.7 us
  blocking collectives  43.3 us (50%)
  starting transfers between devices  20.7 us (24%)
  waiting for transfers between devices  13 us (15%)
  local copies, waits for them, and re-layouts  4.54 us (5%)
  Pallas kernels  4.05 us (5%)
    all_to_all x1, blocking collectives, shards(): lax.all_to_all(packed.reshape(n_seq, 2, total), 'seq', 0, 0, tiled=True)  30.4 us
    all_to_all x1, blocking collectives, shards(): lax.all_to_all(part.reshape(n_doc, per_owner, cols), 'seq', 0, 0, tiled=T...  12.9 us
    all_to_all x1, starting transfers between devices, shards(): lax.all_to_all(jnp.broadcast_to(w_proj.reshape(1, 2, depth // 2, cols), (...  11 us
    ppermute x1, waiting for transfers between devices, shards(): other = lax.ppermute(have, 'doc', [(i, i ^ 1) for i in range(n_doc)])  6.91 us
    all_to_all x1, starting transfers between devices, shards(): lax.all_to_all(rows, 'seq', 0, 0, tiled=True, axis_index_groups=groups)  4.13 us
    all_to_all x1, waiting for transfers between devices, shards(): lax.all_to_all(jnp.broadcast_to(w_proj.reshape(1, 2, depth // 2, cols), (...  3.76 us
    ppermute x1, starting transfers between devices, shards(): other = lax.ppermute(have, 'seq', [(i, i ^ 1) for i in range(n_seq)])  3.41 us
    unnamed x8, local copies, waits for them, and re-layouts  2.75 us
  transfers between devices with their start and end apart: 4, of which 4 were waited for; matrix products, arithmetic and copies ran while one was open for 0% of the time, Pallas kernels for 1%

profile of v2, /device:TPU:1, one launch (start us, length us, event | category | flops | bytes accessed | tf_op | source)
XLA Modules:
  0.0 85.7 jit_solution(11900931712727532760)
XLA Ops:
  0.0 1.4 %broadcast_in_dim.11 = bf16[4,2,8,512]{3,2,1,0:T(8,128)(2,1)} broadcast(bf16[2,8,512]{2,1,0:T(8,128)(2,1)} %bitcast.11), dimensions={1,2,3} | broadcast | bytes 81920 | tf_op jit(solution)/shard_map/broadcast_in_dim | solution.py:116
  1.4 0.0 copy-start.2
  1.4 11.0 %all-to-all-start = ((bf16[8,8,512]{2,1,0:T(8,128)(2,1)}), bf16[8,8,512]{2,1,0:T(8,128)(2,1)S(1)}, u32[]{:S(2)}, u32[]{:S(2)}) async-start(bf16[8,8,512]{2,1,0:T(8,128)(2,1)} %bitcast.3), calls=%async_computation | async-start | bytes 131072 | tf_op jit(solution)/shard_map/all_to_all | solution.py:115
  12.3 0.0 copy-start.3
  12.3 0.0 copy-done.2
  12.4 0.7 copy-done.3
  13.0 0.0 copy-start
  13.0 1.0 %copy-done = bf16[1,256,1024]{2,1,0:T(8,128)(2,1)S(1)} copy-done((bf16[1,256,1024]{2,1,0:T(8,128)(2,1)S(1)}, bf16[1,256,1024]{2,1,0:T(8,128)(2,1)}, u32[]{:S(2)}) %copy-start) | copy-done | bytes 524312
  14.1 0.0 copy-start.1
  14.1 1.0 %copy-done.1 = bf16[1,256,1024]{2,1,0:T(8,128)(2,1)S(1)} copy-done((bf16[1,256,1024]{2,1,0:T(8,128)(2,1)S(1)}, bf16[1,256,1024]{2,1,0:T(8,128)(2,1)}, u32[]{:S(2)}) %copy-start.1) | copy-done | bytes 524312
  15.1 0.7 word_sums.1.sums_ref
  15.8 3.8 %all-to-all-done.w_ref = bf16[8,8,512]{2,1,0:T(8,128)(2,1)S(1)} async-done(((bf16[8,8,512]{2,1,0:T(8,128)(2,1)}), bf16[8,8,512]{2,1,0:T(8,128)(2,1)S(1)}, u32[]{:S(2)}, u32[]{:S(2)}) %all-to-all-start) | async-done | bytes 65568 | tf_op jit(solution)/shard_map/all_to_all | solution.py:115
  19.6 0.2 pack.1
  19.8 0.2 reshape.18
  20.0 30.4 %all_to_all.20 = bf16[64,2,2176]{2,1,0:T(2,128)(2,1)S(1)} all-to-all(bf16[64,2,2176]{2,1,0:T(2,128)(2,1)S(1)} %reshape.18), channel_id=1, replica_groups=mesh['seq'=64,'doc'=8] {'seq'}, dimensions={0} | all-to-all | bytes 1114112 | tf_op jit(solution)/shard_map/all_to_all | solution.py:145
  50.4 0.2 reshape.19.refs_0_
  50.6 1.5 %own_rows.1 = bf16[8,64,1024]{2,1,0:T(8,128)(2,1)} custom-call(bf16[128,2176]{1,0:T(8,128)(2,1)S(1)} %reshape.19.refs_0_), custom_call_target="tpu_custom_call" | custom-call | flops 20000000 | bytes 1500000 | tf_op jit(solution)/shard_map/own_rows/pallas_call | solution.py:149
  52.1 4.1 %all-to-all-start.2 = ((bf16[8,64,1024]{2,1,0:T(8,128)(2,1)}), bf16[8,64,1024]{2,1,0:T(8,128)(2,1)S(1)}, u32[]{:S(2)}, u32[]{:S(2)}) async-start(bf16[8,64,1024]{2,1,0:T(8,128)(2,1)} %own_rows.1), calls=%async_computation.2 | async-start | bytes 2097152 | tf_op jit(solution)/shard_map/all_to_all | solution.py:156
  56.3 2.2 %collective-permute-start = (bf16[128,1024]{1,0:T(8,128)(2,1)S(1)}, bf16[128,1024]{1,0:T(8,128)(2,1)S(1)}, u32[]{:S(2)}, u32[]{:S(2)}) collective-permute-start(bf16[128,1024]{1,0:T(8,128)(2,1)S(1)} %slice.4), channel_id=1, source_target_pairs={{0,1},{1,0},{2,3},{3,2},{4,5},{5,4},{6,7},{7,6},{8,9},{9,8},{10,11... | collective-permute-start | bytes 786440 | tf_op jit(solution)/shard_map/ppermute | solution.py:159
  58.5 6.9 %collective-permute-done = bf16[128,1024]{1,0:T(8,128)(2,1)S(1)} collective-permute-done((bf16[128,1024]{1,0:T(8,128)(2,1)S(1)}, bf16[128,1024]{1,0:T(8,128)(2,1)S(1)}, u32[]{:S(2)}, u32[]{:S(2)}) %collective-permute-start) | collective-permute-done | bytes 262176 | tf_op jit(solution)/shard_map/ppermute | solution.py:159
  65.4 3.4 %collective-permute-start.1 = (bf16[256,1024]{1,0:T(8,128)(2,1)S(1)}, bf16[256,1024]{1,0:T(8,128)(2,1)S(1)}, u32[]{:S(2)}, u32[]{:S(2)}) collective-permute-start(bf16[256,1024]{1,0:T(8,128)(2,1)S(1)} %pad_maximum_fusion.refs_1_), channel_id=1, source_target_pairs={{0,8},{8,0},{16,24},{24,16},{32,40},{40,32},{48,56},{56,48},{64,72... | collective-permute-start | bytes 1572872 | tf_op jit(solution)/shard_map/ppermute | solution.py:161
  68.8 1.5 %collective-permute-done.1.refs_2_ = bf16[256,1024]{1,0:T(8,128)(2,1)S(1)} collective-permute-done((bf16[256,1024]{1,0:T(8,128)(2,1)S(1)}, bf16[256,1024]{1,0:T(8,128)(2,1)S(1)}, u32[]{:S(2)}, u32[]{:S(2)}) %collective-permute-start.1) | collective-permute-done | bytes 524320 | tf_op jit(solution)/shard_map/ppermute | solution.py:161
  70.4 0.9 all-to-all-done.2
  71.2 0.8 project.1
  72.0 12.9 %all_to_all.21.back_ref = bf16[8,64,512]{2,1,0:T(8,128)(2,1)S(1)} all-to-all(bf16[8,64,512]{2,1,0:T(8,128)(2,1)S(1)} %bitcast.8), channel_id=1, replica_groups={{0,16,32,48,64,80,96,112},{8,24,40,56,72,88,104,120},{128,144,160,176,1..., dimensions={0} | all-to-all | bytes 1048576 | tf_op jit(solution)/shard_map/all_to_all | solution.py:172
  84.9 0.8 lay_out.1
  (2 shorter events, 0.1 us)
Async XLA Ops:
  1.4 11.0 %copy-start.2 = (s32[1,4096]{1,0:T(1,128)S(1)}, s32[1,4096]{1,0:T(1,128)}, u32[]{:S(2)}) copy-start(s32[1,4096]{1,0:T(1,128)} %refs_1_.1) | copy-start | bytes 49156
  1.4 18.2 %all-to-all-start = ((bf16[8,8,512]{2,1,0:T(8,128)(2,1)}), bf16[8,8,512]{2,1,0:T(8,128)(2,1)S(1)}, u32[]{:S(2)}, u32[]{:S(2)}) async-start(bf16[8,8,512]{2,1,0:T(8,128)(2,1)} %bitcast.3), calls=%async_computation | async-start | bytes 131072 | tf_op jit(solution)/shard_map/all_to_all | solution.py:115
  12.3 0.7 copy-start.3
  13.0 1.0 %copy-start = (bf16[1,256,1024]{2,1,0:T(8,128)(2,1)S(1)}, bf16[1,256,1024]{2,1,0:T(8,128)(2,1)}, u32[]{:S(2)}) copy-start(bf16[1,256,1024]{2,1,0:T(8,128)(2,1)} %param.5) | copy-start | bytes 1572868
  14.1 1.0 %copy-start.1 = (bf16[1,256,1024]{2,1,0:T(8,128)(2,1)S(1)}, bf16[1,256,1024]{2,1,0:T(8,128)(2,1)}, u32[]{:S(2)}) copy-start(bf16[1,256,1024]{2,1,0:T(8,128)(2,1)} %param.6) | copy-start | bytes 1572868
  52.1 19.1 %all-to-all-start.2 = ((bf16[8,64,1024]{2,1,0:T(8,128)(2,1)}), bf16[8,64,1024]{2,1,0:T(8,128)(2,1)S(1)}, u32[]{:S(2)}, u32[]{:S(2)}) async-start(bf16[8,64,1024]{2,1,0:T(8,128)(2,1)} %own_rows.1), calls=%async_computation.2 | async-start | bytes 2097152 | tf_op jit(solution)/shard_map/all_to_all | solution.py:156
  56.3 9.1 %collective-permute-start = (bf16[128,1024]{1,0:T(8,128)(2,1)S(1)}, bf16[128,1024]{1,0:T(8,128)(2,1)S(1)}, u32[]{:S(2)}, u32[]{:S(2)}) collective-permute-start(bf16[128,1024]{1,0:T(8,128)(2,1)S(1)} %slice.4), channel_id=1, source_target_pairs={{0,1},{1,0},{2,3},{3,2},{4,5},{5,4},{6,7},{7,6},{8,9},{9,8},{10,11... | collective-permute-start | bytes 786440 | tf_op jit(solution)/shard_map/ppermute | solution.py:159
  65.4 4.9 %collective-permute-start.1 = (bf16[256,1024]{1,0:T(8,128)(2,1)S(1)}, bf16[256,1024]{1,0:T(8,128)(2,1)S(1)}, u32[]{:S(2)}, u32[]{:S(2)}) collective-permute-start(bf16[256,1024]{1,0:T(8,128)(2,1)S(1)} %pad_maximum_fusion.refs_1_), channel_id=1, source_target_pairs={{0,8},{8,0},{16,24},{24,16},{32,40},{40,32},{48,56},{56,48},{64,72... | collective-permute-start | bytes 1572872 | tf_op jit(solution)/shard_map/ppermute | solution.py:161

commit v3 on v2

v3 whole, which is shorter than its diff:
```python
import jax
import jax.numpy as jnp
from jax import lax
from jax.experimental import pallas as pl
from jax.experimental.pallas import tpu as pltpu
from jax.sharding import PartitionSpec as P


inv_root_two = 0.7071067811865476
inv_root_tau = 0.3989422804014327
BF16 = jnp.bfloat16
F32 = jnp.float32
LANES = 128


def slope_of(value):
    return (
        0.5 * (1.0 + lax.erf(value * inv_root_two))
        + value * jnp.exp(-0.5 * value * value) * inv_root_tau
    )


def word_sums_kernel(n_seq, word_hbm, owner_hbm, grad_hbm, pre_hbm, keep_ref, send_ref, *scratch):
    word_ref, owner_ref, grad_ref, pre_ref, small_sem, grad_sem, pre_sem = scratch
    half = n_seq
    width = grad_ref.shape[1]
    step = 2 * LANES
    chunks = width // step
    small = [
        pltpu.make_async_copy(word_hbm, word_ref, small_sem.at[0]),
        pltpu.make_async_copy(owner_hbm.at[:, :LANES], owner_ref, small_sem.at[1]),
    ]
    large = []
    for copy in small:
        copy.start()
    for chunk in range(chunks):
        cols = pl.ds(chunk * step, step)
        large.append(
            (
                pltpu.make_async_copy(pre_hbm.at[:, cols], pre_ref.at[:, cols], pre_sem.at[chunk]),
                pltpu.make_async_copy(grad_hbm.at[:, cols], grad_ref.at[:, cols], grad_sem.at[chunk]),
            )
        )
        for copy in large[-1]:
            copy.start()
    source = lax.broadcasted_iota(jnp.int32, (step, step), 0)
    target = lax.broadcasted_iota(jnp.int32, (step, step), 1)
    moved = (
        source // 16 % 2 * 128
        + source // 8 % 2 * 64
        + source // 2 % 4 * 16
        + source // 32 * 2
        + source % 2
    )
    order = jnp.where(moved == target, 1.0, 0.0).astype(BF16)
    core = lax.axis_index("seq") % 2
    row = lax.broadcasted_iota(jnp.int32, (2 * half, LANES), 0)
    lane = lax.broadcasted_iota(jnp.int32, (2 * half, LANES), 1)
    owner = row % half // 2 * 2 + (core ^ row // half)
    for copy in small:
        copy.wait()
    words = word_ref[...]
    rank = words // n_seq
    owned = (owner_ref[...] == owner) & (lane < n_seq)
    remainder = jnp.sum(jnp.where(owned, lane, 0).astype(F32), axis=1, keepdims=True)
    parity = lax.broadcasted_iota(jnp.int32, (2 * half, 1), 0) % 2
    match = (words % n_seq == remainder.astype(jnp.int32)) & (rank % 2 == parity)
    ids = jnp.max(jnp.where(match, rank, 0).astype(F32), axis=1, keepdims=True)
    picks = jnp.where(match, 1.0, 0.0).astype(BF16)
    wide = jnp.broadcast_to(ids, (2 * half, LANES)).astype(BF16)
    keep_ref[:, width:] = wide[:half]
    send_ref[:, width:] = wide[half:]
    for chunk in range(chunks):
        cols = slice(chunk * step, (chunk + 1) * step)
        for copy in large[chunk]:
            copy.wait()
        g_pre = (grad_ref[:, cols].astype(F32) * slope_of(pre_ref[:, cols].astype(F32))).astype(BF16)
        summed = jnp.dot(picks, g_pre, preferred_element_type=F32).astype(BF16)
        summed = jnp.dot(summed, order, preferred_element_type=F32).astype(BF16)
        keep_ref[:, cols] = summed[:half]
        send_ref[:, cols] = summed[half:]


def pack_kernel(keep_ref, other_ref, w_ref, out_ref):
    rows, width = keep_ref.shape
    blocks, depth, cols = w_ref.shape
    out_ref[:, :width] = keep_ref[...]
    out_ref[:, width : 2 * width] = other_ref[...]
    out_row = lax.broadcasted_iota(jnp.int32, (rows, blocks * depth), 0)
    w_row = lax.broadcasted_iota(jnp.int32, (rows, blocks * depth), 1)
    first = (out_row // 8 % 2 * 4 + out_row // 2 % 4) * depth + out_row % 2
    flat = w_ref[...].astype(F32).reshape(blocks * depth, cols).astype(BF16)
    for h in range(depth // 2):
        chosen = jnp.where(w_row == first + 2 * h, 1.0, 0.0).astype(BF16)
        at = 2 * width + h * cols
        out_ref[:, at : at + cols] = jnp.dot(
            chosen, flat, preferred_element_type=F32
        ).astype(BF16)


def own_rows_kernel(per_owner, width, got_ref, out_ref):
    slots = got_ref.shape[0]
    diagonal = lax.broadcasted_iota(jnp.int32, (slots, LANES), 0) == lax.broadcasted_iota(
        jnp.int32, (slots, LANES), 1
    )
    rows = lax.broadcasted_iota(jnp.int32, (per_owner, slots), 0)
    summed = None
    for at in (0, width + LANES):
        wide = got_ref[:, at + width : at + width + LANES].astype(F32)
        ids = jnp.sum(jnp.where(diagonal, wide, 0.0), axis=0, keepdims=True)[:, :slots]
        picks = jnp.where(rows == ids.astype(jnp.int32), 1.0, 0.0).astype(BF16)
        part = jnp.dot(picks, got_ref[:, at : at + width], preferred_element_type=F32)
        summed = part if summed is None else summed + part
    summed = summed.astype(BF16)
    for copy in range(out_ref.shape[0]):
        out_ref[copy] = summed


def project_kernel(rows_ref, mine_ref, theirs_ref, out_ref, w_ref):
    cols = w_ref.shape[1]
    parts = mine_ref.shape[1] // cols
    half = mine_ref.shape[0] // 2
    core = lax.axis_index("seq") % 2
    plane = lax.axis_index("doc") % 2
    for c, source in enumerate((mine_ref, theirs_ref)):
        for z in range(2):
            place = (core ^ c) * 128 + (plane ^ z) * 64
            for tile in range(half // 16):
                at = z * half + tile * 16
                for h in range(parts):
                    start = pl.multiple_of(tile * 256 + h * 16 + place, 16)
                    w_ref[pl.ds(start, 16), :] = source[at : at + 16, h * cols : (h + 1) * cols]
    out_ref[...] = jnp.dot(rows_ref[...], w_ref[...], preferred_element_type=F32).astype(BF16)


def lay_out_kernel(back_ref, out_ref):
    cols = back_ref.shape[2]
    for block in range(back_ref.shape[0]):
        out_ref[:, block * cols : (block + 1) * cols] = back_ref[block]


def step(grad_out, pre_act, word_of, word_owner, w_proj):
    n_seq = lax.axis_size("seq")
    n_doc = lax.axis_size("doc")
    n_chip = n_seq // 2
    bytes_here, width = grad_out.shape[1:]
    per_owner = word_owner.shape[1] // n_seq
    depth, cols = w_proj.shape
    part = width + LANES
    total = 2 * part + depth // 4 * cols
    groups = [
        [32 * y2 + 16 * y1 + 8 * y0 + 2 * x + c for y0 in range(2) for x in range(4)]
        for y2 in range(2)
        for y1 in range(2)
        for c in range(2)
    ]
    same_core = [[2 * chip + c for chip in range(n_chip)] for c in range(2)]
    across = [(i, i ^ 1) for i in range(n_seq)]
    params = pltpu.CompilerParams(vmem_limit_bytes=VMEM_LIMIT)

    w_docs = lax.all_to_all(
        jnp.broadcast_to(
            w_proj.reshape(1, 2, depth // 2, cols), (n_doc // 2, 2, depth // 2, cols)
        ).reshape(n_doc, depth // 2, cols),
        "doc", 0, 0, tiled=True,
    )
    chunks = width // (2 * LANES)
    inputs = [
        pltpu.with_memory_space_constraint(x, pltpu.HBM)
        for x in (word_of, word_owner, grad_out[0], pre_act[0])
    ]
    keep, send = pl.pallas_call(
        lambda *refs: word_sums_kernel(n_seq, *refs),
        out_shape=[jax.ShapeDtypeStruct((n_seq, part), BF16)] * 2,
        in_specs=[pl.BlockSpec(memory_space=pltpu.HBM)] * 4,
        scratch_shapes=[
            pltpu.VMEM((1, bytes_here), jnp.int32),
            pltpu.VMEM((1, LANES), jnp.int32),
            pltpu.VMEM((bytes_here, width), BF16),
            pltpu.VMEM((bytes_here, width), BF16),
            pltpu.SemaphoreType.DMA((2,)),
            pltpu.SemaphoreType.DMA((chunks,)),
            pltpu.SemaphoreType.DMA((chunks,)),
        ],
        compiler_params=params,
        cost_estimate=pl.CostEstimate(flops=20_000_000, bytes_accessed=3_000_000, transcendentals=500_000),
        name="word_sums",
    )(*inputs)
    other = lax.ppermute(send, "seq", across)
    packed = pl.pallas_call(
        pack_kernel,
        out_shape=jax.ShapeDtypeStruct((n_seq, total), BF16),
        compiler_params=params,
        cost_estimate=pl.CostEstimate(flops=20_000_000, bytes_accessed=1_000_000, transcendentals=0),
        name="pack",
    )(keep, other, w_docs)
    got = lax.all_to_all(
        packed.reshape(n_chip, 2, total), "seq", 0, 0, tiled=True, axis_index_groups=same_core
    ).reshape(n_seq, total)

    rows = pl.pallas_call(
        lambda *refs: own_rows_kernel(per_owner, width, *refs),
        out_shape=jax.ShapeDtypeStruct((n_doc, per_owner, width), BF16),
        compiler_params=params,
        cost_estimate=pl.CostEstimate(flops=20_000_000, bytes_accessed=1_500_000, transcendentals=0),
        name="own_rows",
    )(got)
    rows = lax.all_to_all(rows, "seq", 0, 0, tiled=True, axis_index_groups=groups)

    mine = got[:, 2 * part :]
    theirs = lax.ppermute(mine, "doc", [(i, i ^ 1) for i in range(n_doc)])
    mine = jnp.concatenate([mine, theirs], axis=0)
    theirs = lax.ppermute(mine, "seq", across)

    out = pl.pallas_call(
        project_kernel,
        out_shape=jax.ShapeDtypeStruct((n_doc * per_owner, cols), BF16),
        scratch_shapes=[pltpu.VMEM((width, cols), BF16)],
        compiler_params=params,
        cost_estimate=pl.CostEstimate(flops=600_000_000, bytes_accessed=2_500_000, transcendentals=0),
        name="project",
    )(rows.reshape(n_doc * per_owner, width), mine, theirs)
    back = lax.all_to_all(
        out.reshape(n_doc, per_owner, cols), "seq", 0, 0, tiled=True, axis_index_groups=groups
    )
    out = pl.pallas_call(
        lay_out_kernel,
        out_shape=jax.ShapeDtypeStruct((per_owner, n_doc * cols), BF16),
        compiler_params=params,
        name="lay_out",
    )(back)
    return out[None]


VMEM_LIMIT = 16 * 1024 * 1024


def solution(mesh):
    return jax.shard_map(
        step,
        mesh=mesh,
        in_specs=(
            P("doc", "seq", None),
            P("doc", "seq", None),
            P("doc", "seq"),
            P("doc", None),
            P("seq", "doc"),
        ),
        out_specs=P("doc", "seq", None),
        check_vma=False,
    )
```

time: 86.3 us -> 85.6 us (level)
  blocking collectives: 43.3 us -> 51 us
  waiting for transfers between devices: 13 us -> 6.66 us
  local copies, waits for them, and re-layouts: 4.54 us -> 0.45 us
  Pallas kernels: 4.05 us -> 5.99 us
    ppermute x2 -> x3, starting transfers between devices: 5.6 us -> 16.8 us  [the longest x1 8.75 us: step(): other = lax.ppermute(send, 'seq', across)]
    all_to_all x2 -> x1, starting transfers between devices: 15.1 us -> 4.26 us  [step(): lax.all_to_all(rows, 'seq', 0, 0, tiled=True, axis_index_groups=groups)]
    all_to_all x2 -> x3, blocking collectives: 43.3 us -> 51 us  [the longest x1 25.3 us: step(): lax.all_to_all(packed.reshape(n_chip, 2, total), 'seq', 0, 0, tiled=True,...]
    all_to_all x2 -> x1, waiting for transfers between devices: 4.62 us -> 0.01 us  [step(): lax.all_to_all(rows, 'seq', 0, 0, tiled=True, axis_index_groups=groups)]
    unnamed x8 -> x2, local copies, waits for them, and re-layouts: 2.75 us -> 0.01 us
    pallas_call x5, Pallas kernels: 4.05 us -> 5.99 us  [the longest x1 2.91 us: step(): pl.pallas_call(lambda *refs: word_sums_kernel(n_seq, *refs), out_shape=[j...]
    ppermute x2 -> x3, waiting for transfers between devices: 8.43 us -> 6.66 us  [the longest x1 5.14 us: step(): theirs = lax.ppermute(mine, 'doc', [(i, i ^ 1) for i in range(n_doc)])]
    broadcast_in_dim x1, local copies, waits for them, and re-layouts: 1.35 us -> 0.01 us  [step(): jnp.broadcast_to(w_proj.reshape(1, 2, depth // 2, cols), (n_doc // 2, 2,...]
  transfers between devices with their start and end apart: 4 -> 4, of which waited for: 4 -> 2; matrix products, arithmetic and copies ran while one was open for 0% -> 0% of each run, Pallas kernels for 1% -> 0%
where the time goes in v3:
time: 85.6 us; the launch traced here: 85.2 us
  blocking collectives  51 us (60%)
  starting transfers between devices  21 us (25%)
  waiting for transfers between devices  6.66 us (8%)
  Pallas kernels  5.99 us (7%)
    all_to_all x1, blocking collectives, step(): lax.all_to_all(packed.reshape(n_chip, 2, total), 'seq', 0, 0, tiled=True,...  25.3 us
    all_to_all x1, blocking collectives, step(): lax.all_to_all(out.reshape(n_doc, per_owner, cols), 'seq', 0, 0, tiled=Tr...  14 us
    all_to_all x1, blocking collectives, step(): lax.all_to_all(jnp.broadcast_to(w_proj.reshape(1, 2, depth // 2, cols), (...  11.6 us
    ppermute x1, starting transfers between devices, step(): other = lax.ppermute(send, 'seq', across)  8.75 us
    ppermute x1, starting transfers between devices, step(): theirs = lax.ppermute(mine, 'seq', across)  5.74 us
    ppermute x1, waiting for transfers between devices, step(): theirs = lax.ppermute(mine, 'doc', [(i, i ^ 1) for i in range(n_doc)])  5.14 us
    all_to_all x1, starting transfers between devices, step(): lax.all_to_all(rows, 'seq', 0, 0, tiled=True, axis_index_groups=groups)  4.26 us
    pallas_call x1, Pallas kernels, step(): pl.pallas_call(lambda *refs: word_sums_kernel(n_seq, *refs), out_shape=[j...  2.91 us
  transfers between devices with their start and end apart: 4, of which 2 were waited for; matrix products, arithmetic and copies ran while one was open for 0% of the time, Pallas kernels for 0%

profile of v3, /device:TPU:1, one launch (start us, length us, event | category | flops | bytes accessed | tf_op | source)
XLA Modules:
  0.0 85.2 jit_solution(9469777282153878033)
XLA Ops:
  0.0 0.0 copy-start
  0.0 2.9 %word_sums.1 = (bf16[64,1152]{1,0:T(8,128)(2,1)S(1)}, bf16[64,1152]{1,0:T(8,128)(2,1)S(1)}) custom-call(s32[1,256]{1,0:T(1,128)} %refs_0_.1, s32[1,4096]{1,0:T(1,128)} %refs_1_.1, bf16[256,1024]{1,0:T(8,128)(2,1)} %bitcast.9, bf16[256,1024]{1,0:T(8,128)(2,1)} %bitcast.10), custom_call_target="tpu_custom_call" | custom-call | flops 20000000 | bytes 3000000 | tf_op jit(solution)/shard_map/word_sums/pallas_call | solution.py:172
  2.9 8.7 %collective-permute-start = (bf16[64,1152]{1,0:T(8,128)(2,1)S(1)}, bf16[64,1152]{1,0:T(8,128)(2,1)S(1)}, u32[]{:S(2)}, u32[]{:S(2)}) collective-permute-start(bf16[64,1152]{1,0:T(8,128)(2,1)S(1)} %get-tuple-element.8), channel_id=1, source_target_pairs={{0,8},{8,0},{16,24},{24,16},{32,40},{40,32},{48,56},{56,48},{64,72... | collective-permute-start | bytes 442376 | tf_op jit(solution)/shard_map/ppermute | solution.py:189
  11.7 0.0 copy-done
  11.7 11.6 %all_to_all.20.w_ref = bf16[8,8,512]{2,1,0:T(8,128)(2,1)S(1)} all-to-all(bf16[8,8,512]{2,1,0:T(8,128)(2,1)S(1)} %bitcast.11), channel_id=1, replica_groups=mesh['seq'=64,'doc'=8] {'doc'}, dimensions={0} | all-to-all | bytes 131072 | tf_op jit(solution)/shard_map/all_to_all | solution.py:161
  23.3 0.0 collective-permute-done.other_ref
  23.3 0.2 pack.1
  23.6 0.2 reshape.18
  23.8 25.3 %all_to_all.21 = bf16[32,2,4352]{2,1,0:T(2,128)(2,1)S(1)} all-to-all(bf16[32,2,4352]{2,1,0:T(2,128)(2,1)S(1)} %reshape.18), channel_id=1, replica_groups={{0,16,32,48,64,80,96,112,128,144,160,176,192,208,224,240,256,272,288,30..., dimensions={0} | all-to-all | bytes 1114112 | tf_op jit(solution)/shard_map/all_to_all | solution.py:197
  49.1 0.2 reshape.19.refs_0_
  49.3 1.3 %own_rows.1 = bf16[8,64,1024]{2,1,0:T(8,128)(2,1)} custom-call(bf16[64,4352]{1,0:T(8,128)(2,1)S(1)} %reshape.19.refs_0_), custom_call_target="tpu_custom_call" | custom-call | flops 20000000 | bytes 1500000 | tf_op jit(solution)/shard_map/own_rows/pallas_call | solution.py:201
  50.6 4.3 %all-to-all-start.2 = ((bf16[8,64,1024]{2,1,0:T(8,128)(2,1)}), bf16[8,64,1024]{2,1,0:T(8,128)(2,1)S(1)}, u32[]{:S(2)}, u32[]{:S(2)}) async-start(bf16[8,64,1024]{2,1,0:T(8,128)(2,1)} %own_rows.1), calls=%async_computation.2 | async-start | bytes 2097152 | tf_op jit(solution)/shard_map/all_to_all | solution.py:208
  54.8 2.3 %collective-permute-start.1 = (bf16[64,2048]{1,0:T(8,128)(2,1)S(1)}, bf16[64,2048]{1,0:T(8,128)(2,1)S(1)}, u32[]{:S(2)}, u32[]{:S(2)}) collective-permute-start(bf16[64,2048]{1,0:T(8,128)(2,1)S(1)} %slice.4), channel_id=1, source_target_pairs={{0,1},{1,0},{2,3},{3,2},{4,5},{5,4},{6,7},{7,6},{8,9},{9,8},{10,11... | collective-permute-start | bytes 786440 | tf_op jit(solution)/shard_map/ppermute | solution.py:211
  57.1 5.1 %collective-permute-done.1 = bf16[64,2048]{1,0:T(8,128)(2,1)S(1)} collective-permute-done((bf16[64,2048]{1,0:T(8,128)(2,1)S(1)}, bf16[64,2048]{1,0:T(8,128)(2,1)S(1)}, u32[]{:S(2)}, u32[]{:S(2)}) %collective-permute-start.1) | collective-permute-done | bytes 262176 | tf_op jit(solution)/shard_map/ppermute | solution.py:211
  62.3 5.7 %collective-permute-start.2 = (bf16[128,2048]{1,0:T(8,128)(2,1)S(1)}, bf16[128,2048]{1,0:T(8,128)(2,1)S(1)}, u32[]{:S(2)}, u32[]{:S(2)}) collective-permute-start(bf16[128,2048]{1,0:T(8,128)(2,1)S(1)} %pad_maximum_fusion.mine_ref), channel_id=1, source_target_pairs={{0,8},{8,0},{16,24},{24,16},{32,40},{40,32},{48,56},{56,48},{64,72... | collective-permute-start | bytes 1572872 | tf_op jit(solution)/shard_map/ppermute | solution.py:213
  68.0 1.5 %collective-permute-done.2.theirs_ref = bf16[128,2048]{1,0:T(8,128)(2,1)S(1)} collective-permute-done((bf16[128,2048]{1,0:T(8,128)(2,1)S(1)}, bf16[128,2048]{1,0:T(8,128)(2,1)S(1)}, u32[]{:S(2)}, u32[]{:S(2)}) %collective-permute-start.2) | collective-permute-done | bytes 524320 | tf_op jit(solution)/shard_map/ppermute | solution.py:213
  69.6 0.0 all-to-all-done.2
  69.6 0.8 project.1
  70.3 14.0 %all_to_all.22.back_ref = bf16[8,64,512]{2,1,0:T(8,128)(2,1)S(1)} all-to-all(bf16[8,64,512]{2,1,0:T(8,128)(2,1)S(1)} %bitcast.8), channel_id=1, replica_groups={{0,16,32,48,64,80,96,112},{8,24,40,56,72,88,104,120},{128,144,160,176,1..., dimensions={0} | all-to-all | bytes 1048576 | tf_op jit(solution)/shard_map/all_to_all | solution.py:223
  84.4 0.8 lay_out.1
  (3 shorter events, 0.1 us)
Async XLA Ops:
  0.0 11.7 %copy-start = (bf16[16,512]{1,0:T(8,128)(2,1)S(1)}, bf16[16,512]{1,0:T(8,128)(2,1)}, u32[]{:S(2)}) copy-start(bf16[16,512]{1,0:T(8,128)(2,1)} %param.9) | copy-start | bytes 49156
  2.9 20.4 %collective-permute-start = (bf16[64,1152]{1,0:T(8,128)(2,1)S(1)}, bf16[64,1152]{1,0:T(8,128)(2,1)S(1)}, u32[]{:S(2)}, u32[]{:S(2)}) collective-permute-start(bf16[64,1152]{1,0:T(8,128)(2,1)S(1)} %get-tuple-element.8), channel_id=1, source_target_pairs={{0,8},{8,0},{16,24},{24,16},{32,40},{40,32},{48,56},{56,48},{64,72... | collective-permute-start | bytes 442376 | tf_op jit(solution)/shard_map/ppermute | solution.py:189
  50.6 19.0 %all-to-all-start.2 = ((bf16[8,64,1024]{2,1,0:T(8,128)(2,1)}), bf16[8,64,1024]{2,1,0:T(8,128)(2,1)S(1)}, u32[]{:S(2)}, u32[]{:S(2)}) async-start(bf16[8,64,1024]{2,1,0:T(8,128)(2,1)} %own_rows.1), calls=%async_computation.2 | async-start | bytes 2097152 | tf_op jit(solution)/shard_map/all_to_all | solution.py:208
  54.8 7.4 %collective-permute-start.1 = (bf16[64,2048]{1,0:T(8,128)(2,1)S(1)}, bf16[64,2048]{1,0:T(8,128)(2,1)S(1)}, u32[]{:S(2)}, u32[]{:S(2)}) collective-permute-start(bf16[64,2048]{1,0:T(8,128)(2,1)S(1)} %slice.4), channel_id=1, source_target_pairs={{0,1},{1,0},{2,3},{3,2},{4,5},{5,4},{6,7},{7,6},{8,9},{9,8},{10,11... | collective-permute-start | bytes 786440 | tf_op jit(solution)/shard_map/ppermute | solution.py:211
  62.3 7.3 %collective-permute-start.2 = (bf16[128,2048]{1,0:T(8,128)(2,1)S(1)}, bf16[128,2048]{1,0:T(8,128)(2,1)S(1)}, u32[]{:S(2)}, u32[]{:S(2)}) collective-permute-start(bf16[128,2048]{1,0:T(8,128)(2,1)S(1)} %pad_maximum_fusion.mine_ref), channel_id=1, source_target_pairs={{0,8},{8,0},{16,24},{24,16},{32,40},{40,32},{48,56},{56,48},{64,72... | collective-permute-start | bytes 1572872 | tf_op jit(solution)/shard_map/ppermute | solution.py:213

commit v4 on v3

v4 whole, which is shorter than its diff:
```python
import jax
import jax.numpy as jnp
from jax import lax
from jax.experimental import pallas as pl
from jax.experimental.pallas import tpu as pltpu
from jax.sharding import PartitionSpec as P


inv_root_two = 0.7071067811865476
inv_root_tau = 0.3989422804014327
BF16 = jnp.bfloat16
F32 = jnp.float32
LANES = 128


def slope_of(value):
    return (
        0.5 * (1.0 + lax.erf(value * inv_root_two))
        + value * jnp.exp(-0.5 * value * value) * inv_root_tau
    )


def load_kernel(word_hbm, owner_hbm, grad_hbm, pre_hbm, w_hbm, word_ref, owner_ref, grad_ref, pre_ref, sent_hbm, w_ref, sems):
    half = w_ref.shape[0] // 2
    first = [pltpu.make_async_copy(w_hbm, w_ref, sems.at[0])]
    loads = [
        pltpu.make_async_copy(word_hbm, word_ref, sems.at[1]),
        pltpu.make_async_copy(owner_hbm.at[:, :LANES], owner_ref, sems.at[2]),
        pltpu.make_async_copy(pre_hbm, pre_ref, sems.at[3]),
        pltpu.make_async_copy(grad_hbm, grad_ref, sems.at[4]),
    ]
    for copy in first:
        copy.start()
    for copy in loads:
        copy.start()
    for copy in first:
        copy.wait()
    stores = [
        pltpu.make_async_copy(w_ref.at[pl.ds(d % 2 * half, half), :], sent_hbm.at[i], sems.at[5 + i])
        for i, d in enumerate(DOC_ORDER)
    ]
    for copy in stores:
        copy.start()
    for copy in loads + stores:
        copy.wait()


def word_sums_kernel(n_seq, word_ref, owner_ref, grad_ref, pre_ref, keep_ref, send_ref):
    half = n_seq
    width = grad_ref.shape[1]
    step = 2 * LANES
    chunks = width // step
    source = lax.broadcasted_iota(jnp.int32, (step, step), 0)
    target = lax.broadcasted_iota(jnp.int32, (step, step), 1)
    moved = (
        source // 16 % 2 * 128
        + source // 8 % 2 * 64
        + source // 2 % 4 * 16
        + (7 - source // 32 if REVERSE_SEQ else source // 32) * 2
        + source % 2
    )
    order = jnp.where(moved == target, 1.0, 0.0).astype(BF16)
    core = lax.axis_index("seq") % 2
    row = lax.broadcasted_iota(jnp.int32, (2 * half, LANES), 0)
    lane = lax.broadcasted_iota(jnp.int32, (2 * half, LANES), 1)
    chip = row % half // 2
    chip = half // 2 - 1 - chip if REVERSE_SEQ else chip
    owner = chip * 2 + (core ^ row // half)
    words = word_ref[...]
    rank = words // n_seq
    owned = (owner_ref[...] == owner) & (lane < n_seq)
    remainder = jnp.sum(jnp.where(owned, lane, 0).astype(F32), axis=1, keepdims=True)
    parity = lax.broadcasted_iota(jnp.int32, (2 * half, 1), 0) % 2
    match = (words % n_seq == remainder.astype(jnp.int32)) & (rank % 2 == parity)
    ids = jnp.max(jnp.where(match, rank, 0).astype(F32), axis=1, keepdims=True)
    picks = jnp.where(match, 1.0, 0.0).astype(BF16)
    wide = jnp.broadcast_to(ids, (2 * half, LANES)).astype(BF16)
    keep_ref[:, width:] = wide[:half]
    send_ref[:, width:] = wide[half:]
    for chunk in range(chunks):
        cols = slice(chunk * step, (chunk + 1) * step)
        g_pre = (grad_ref[:, cols].astype(F32) * slope_of(pre_ref[:, cols].astype(F32))).astype(BF16)
        summed = jnp.dot(picks, g_pre, preferred_element_type=F32).astype(BF16)
        summed = jnp.dot(summed, order, preferred_element_type=F32).astype(BF16)
        keep_ref[:, cols] = summed[:half]
        send_ref[:, cols] = summed[half:]


def pack_kernel(keep_ref, other_ref, w_ref, out_ref):
    rows = keep_ref.shape[0]
    width = keep_ref.shape[1] - LANES
    blocks, depth, cols = w_ref.shape
    out_ref[:, :width] = keep_ref[:, :width]
    out_ref[:, width : 2 * width] = other_ref[:, :width]
    lane = lax.broadcasted_iota(jnp.int32, (rows, LANES), 1)
    ids = [ref[:, width:].astype(F32) for ref in (keep_ref, other_ref)]
    out_ref[:, 2 * width : 2 * width + LANES] = jnp.where(lane < rows, *ids).astype(BF16)
    out_row = lax.broadcasted_iota(jnp.int32, (rows, blocks * depth), 0)
    w_row = lax.broadcasted_iota(jnp.int32, (rows, blocks * depth), 1)
    chip = out_row // 2
    chip = rows // 2 - 1 - chip if REVERSE_SEQ else chip
    block = chip // 4 % 2 * 4 + chip % 4
    place = sum(jnp.where(block == d, i, 0) for i, d in enumerate(DOC_ORDER))
    first = place * depth + out_row % 2
    flat = w_ref[...].astype(F32).reshape(blocks * depth, cols).astype(BF16)
    for h in range(depth // 2):
        chosen = jnp.where(w_row == first + 2 * h, 1.0, 0.0).astype(BF16)
        at = 2 * width + LANES + h * cols
        out_ref[:, at : at + cols] = jnp.dot(
            chosen, flat, preferred_element_type=F32
        ).astype(BF16)


def own_rows_kernel(per_owner, width, got_ref, out_ref):
    slots = got_ref.shape[0]
    slot = lax.broadcasted_iota(jnp.int32, (slots, LANES), 0)
    lane = lax.broadcasted_iota(jnp.int32, (slots, LANES), 1)
    wide = got_ref[:, 2 * width : 2 * width + LANES].astype(F32)
    ids = jnp.sum(jnp.where(slot == lane % slots, wide, 0.0), axis=0, keepdims=True)
    rows = lax.broadcasted_iota(jnp.int32, (per_owner, LANES), 0)
    picks = jnp.where(rows == ids.astype(jnp.int32), 1.0, 0.0).astype(BF16)
    summed = jnp.dot(
        picks[:, :slots], got_ref[:, :width], preferred_element_type=F32
    ) + jnp.dot(picks[:, slots:], got_ref[:, width : 2 * width], preferred_element_type=F32)
    summed = summed.astype(BF16)
    for copy in range(out_ref.shape[0]):
        out_ref[copy] = summed


def project_kernel(rows_ref, mine_ref, theirs_ref, out_ref, w_ref):
    cols = w_ref.shape[1]
    parts = mine_ref.shape[1] // cols
    half = mine_ref.shape[0] // 2
    core = lax.axis_index("seq") % 2
    plane = lax.axis_index("doc") % 2
    for c, source in enumerate((mine_ref, theirs_ref)):
        for z in range(2):
            place = (core ^ c) * 128 + (plane ^ z) * 64
            for tile in range(half // 16):
                at = z * half + tile * 16
                for h in range(parts):
                    to = half // 16 - 1 - tile if REVERSE_SEQ else tile
                    start = pl.multiple_of(to * 256 + h * 16 + place, 16)
                    w_ref[pl.ds(start, 16), :] = source[at : at + 16, h * cols : (h + 1) * cols]
    out_ref[...] = jnp.dot(rows_ref[...], w_ref[...], preferred_element_type=F32).astype(BF16)


def lay_out_kernel(back_ref, out_hbm, sems):
    blocks, _, cols = back_ref.shape
    stores = [
        pltpu.make_async_copy(back_ref.at[i], out_hbm.at[:, pl.ds(i * cols, cols)], sems.at[i])
        for i in range(blocks)
    ]
    for copy in stores:
        copy.start()
    for copy in stores:
        copy.wait()


def step(grad_out, pre_act, word_of, word_owner, w_proj):
    n_seq = lax.axis_size("seq")
    n_doc = lax.axis_size("doc")
    n_chip = n_seq // 2
    bytes_here, width = grad_out.shape[1:]
    per_owner = word_owner.shape[1] // n_seq
    depth, cols = w_proj.shape
    part = width + LANES
    total = 2 * width + LANES + depth // 4 * cols
    groups = [
        [32 * y2 + 16 * y1 + 8 * y0 + 2 * x + c for y0 in range(2) for x in range(4)]
        for y2 in range(2)
        for y1 in range(2)
        for c in range(2)
    ]
    chips = list(range(n_chip))[:: -1 if REVERSE_SEQ else 1]
    same_core = [[2 * chip + c for chip in chips] for c in range(2)]
    across = [(i, i ^ 1) for i in range(n_seq)]
    params = pltpu.CompilerParams(vmem_limit_bytes=VMEM_LIMIT)

    hbm = pl.BlockSpec(memory_space=pltpu.HBM)
    vmem = pl.BlockSpec(memory_space=pltpu.VMEM)
    *inputs, w_sent = pl.pallas_call(
        load_kernel,
        out_shape=[
            jax.ShapeDtypeStruct(word_of.shape, word_of.dtype),
            jax.ShapeDtypeStruct((1, LANES), word_owner.dtype),
            jax.ShapeDtypeStruct((bytes_here, width), BF16),
            jax.ShapeDtypeStruct((bytes_here, width), BF16),
            jax.ShapeDtypeStruct((n_doc, depth // 2, cols), BF16),
        ],
        in_specs=[hbm] * 5,
        out_specs=[vmem] * 4 + [hbm],
        scratch_shapes=[
            pltpu.VMEM((depth, cols), BF16),
            pltpu.SemaphoreType.DMA((5 + n_doc,)),
        ],
        compiler_params=params,
        cost_estimate=pl.CostEstimate(flops=0, bytes_accessed=2_000_000, transcendentals=0),
        name="load",
    )(
        *(
            pltpu.with_memory_space_constraint(x, pltpu.HBM)
            for x in (word_of, word_owner, grad_out[0], pre_act[0], w_proj)
        )
    )
    w_docs = lax.all_to_all(
        w_sent, "doc", 0, 0, tiled=True,
        axis_index_groups=[list(DOC_ORDER)],
    )
    keep, send = pl.pallas_call(
        lambda *refs: word_sums_kernel(n_seq, *refs),
        out_shape=[jax.ShapeDtypeStruct((n_seq, part), BF16)] * 2,
        in_specs=[vmem] * 4,
        out_specs=[vmem] * 2,
        compiler_params=params,
        cost_estimate=pl.CostEstimate(flops=20_000_000, bytes_accessed=3_000_000, transcendentals=500_000),
        name="word_sums",
    )(*inputs)
    other = lax.ppermute(send, "seq", across)
    packed = pl.pallas_call(
        pack_kernel,
        out_shape=jax.ShapeDtypeStruct((n_seq, total), BF16),
        compiler_params=params,
        cost_estimate=pl.CostEstimate(flops=20_000_000, bytes_accessed=1_000_000, transcendentals=0),
        name="pack",
    )(keep, other, w_docs)
    got = lax.all_to_all(
        packed.reshape(n_chip, 2, total), "seq", 0, 0, tiled=True, axis_index_groups=same_core
    ).reshape(n_seq, total)

    rows = pl.pallas_call(
        lambda *refs: own_rows_kernel(per_owner, width, *refs),
        out_shape=jax.ShapeDtypeStruct((n_doc, per_owner, width), BF16),
        compiler_params=params,
        cost_estimate=pl.CostEstimate(flops=20_000_000, bytes_accessed=1_500_000, transcendentals=0),
        name="own_rows",
    )(got)
    rows = lax.all_to_all(rows, "seq", 0, 0, tiled=True, axis_index_groups=groups)

    mine = got[:, 2 * width + LANES :]
    theirs = lax.ppermute(mine, "doc", [(i, i ^ 1) for i in range(n_doc)])
    mine = jnp.concatenate([mine, theirs], axis=0)
    theirs = lax.ppermute(mine, "seq", across)

    out = pl.pallas_call(
        project_kernel,
        out_shape=jax.ShapeDtypeStruct((n_doc * per_owner, cols), BF16),
        scratch_shapes=[pltpu.VMEM((width, cols), BF16)],
        compiler_params=params,
        cost_estimate=pl.CostEstimate(flops=600_000_000, bytes_accessed=2_500_000, transcendentals=0),
        name="project",
    )(rows.reshape(n_doc * per_owner, width), mine, theirs)
    back = lax.all_to_all(
        out.reshape(n_doc, per_owner, cols), "seq", 0, 0, tiled=True, axis_index_groups=groups
    )
    out = pl.pallas_call(
        lay_out_kernel,
        out_shape=jax.ShapeDtypeStruct((per_owner, n_doc * cols), BF16),
        in_specs=[vmem],
        out_specs=hbm,
        scratch_shapes=[pltpu.SemaphoreType.DMA((n_doc,))],
        compiler_params=params,
        name="lay_out",
    )(back)
    return out[None]


DOC_ORDER = (7, 0, 6, 1, 5, 2, 4, 3)
REVERSE_SEQ = True
VMEM_LIMIT = 16 * 1024 * 1024


def solution(mesh):
    return jax.shard_map(
        step,
        mesh=mesh,
        in_specs=(
            P("doc", "seq", None),
            P("doc", "seq", None),
            P("doc", "seq"),
            P("doc", None),
            P("seq", "doc"),
        ),
        out_specs=P("doc", "seq", None),
        check_vma=False,
    )
```

time: 85.6 us -> 81.2 us (0.949)
  blocking collectives: 51 us -> 46.1 us
  starting transfers between devices: 21 us -> 22.6 us
    all_to_all x1, blocking collectives: 25.3 us -> 21.8 us  [step(): lax.all_to_all(packed.reshape(n_chip, 2, total), 'seq', 0, 0, tiled=True,...]
    pallas_call x1, Pallas kernels: 2.91 us -> 0.92 us  [step(): pl.pallas_call(lambda *refs: word_sums_kernel(n_seq, *refs), out_shape=[j...]
    all_to_all x1, starting transfers between devices: 4.26 us -> 5.89 us  [step(): lax.all_to_all(rows, 'seq', 0, 0, tiled=True, axis_index_groups=groups)]
    pallas_call x0 -> x1, Pallas kernels: none -> 1.37 us  [step(): pl.pallas_call(load_kernel, out_shape=[jax.ShapeDtypeStruct(word_of.shape...]
    all_to_all x1, blocking collectives: 11.6 us -> 10.5 us  [step(): lax.all_to_all(w_sent, 'doc', 0, 0, tiled=True, axis_index_groups=[list(D...]
    ppermute x1, starting transfers between devices: 5.74 us -> 4.83 us  [step(): theirs = lax.ppermute(mine, 'seq', across)]
where the time goes in v4:
time: 81.2 us; the launch traced here: 80.8 us
  blocking collectives  46.1 us (57%)
  starting transfers between devices  22.6 us (28%)
  waiting for transfers between devices  6.11 us (8%)
  Pallas kernels  5.5 us (7%)
    all_to_all x1, blocking collectives, step(): lax.all_to_all(packed.reshape(n_chip, 2, total), 'seq', 0, 0, tiled=True,...  21.8 us
    all_to_all x1, blocking collectives, step(): lax.all_to_all(out.reshape(n_doc, per_owner, cols), 'seq', 0, 0, tiled=Tr...  13.8 us
    all_to_all x1, blocking collectives, step(): lax.all_to_all(w_sent, 'doc', 0, 0, tiled=True, axis_index_groups=[list(D...  10.5 us
    ppermute x1, starting transfers between devices, step(): other = lax.ppermute(send, 'seq', across)  8.75 us
    all_to_all x1, starting transfers between devices, step(): lax.all_to_all(rows, 'seq', 0, 0, tiled=True, axis_index_groups=groups)  5.89 us
    ppermute x1, starting transfers between devices, step(): theirs = lax.ppermute(mine, 'seq', across)  4.83 us
    ppermute x1, waiting for transfers between devices, step(): theirs = lax.ppermute(mine, 'doc', [(i, i ^ 1) for i in range(n_doc)])  4.59 us
    ppermute x1, starting transfers between devices, step(): theirs = lax.ppermute(mine, 'doc', [(i, i ^ 1) for i in range(n_doc)])  3.1 us
  transfers between devices with their start and end apart: 4, of which 2 were waited for; matrix products, arithmetic and copies ran while one was open for 0% of the time, Pallas kernels for 0%

profile of v4, /device:TPU:1, one launch (start us, length us, event | category | flops | bytes accessed | tf_op | source)
XLA Modules:
  0.0 80.8 jit_solution(7144874690042536031)
XLA Ops:
  0.0 1.4 %load.1 = (s32[1,256]{1,0:T(1,128)S(1)}, s32[1,128]{1,0:T(1,128)S(1)}, bf16[256,1024]{1,0:T(8,128)(2,1)S(1)}, bf16[256,1024]{1,0:T(8,128)(2,1)S(1)}, bf16[8,8,512]{2,1,0:T(8,128)(2,1)S(1)}) custom-call(s32[1,256]{1,0:T(1,128)} %word_hbm.1, s32[1,4096]{1,0:T(1,128)} %owner_hbm.1, bf16[256,1024]{1,0:T(8,128)(2,1)} %bitcast.7, bf16[256,1024]{1,0:T(8,128)(2,1)} %bitcast.8, ...), custom_call_target="tpu_custom_call" | custom-call | bytes 2000000 | tf_op jit(solution)/shard_map/load/pallas_call | solution.py:182
  1.4 0.9 %word_sums.1 = (bf16[64,1152]{1,0:T(8,128)(2,1)S(1)}, bf16[64,1152]{1,0:T(8,128)(2,1)S(1)}) custom-call(s32[1,256]{1,0:T(1,128)S(1)} %get-tuple-element.12.refs_0_, s32[1,128]{1,0:T(1,128)S(1)} %get-tuple-element.13.refs_1_, bf16[256,1024]{1,0:T(8,128)(2,1)S(1)} %get-tuple-element.14.refs_2_, bf16[256,1024]{1,0:T(8,128)(2,1)S(1)} %get-tuple-element.15.refs_3_), custom_call_target="tpu_custom_call" | custom-call | flops 20000000 | bytes 3000000 | tf_op jit(solution)/shard_map/word_sums/pallas_call | solution.py:210
  2.3 8.7 %collective-permute-start = (bf16[64,1152]{1,0:T(8,128)(2,1)S(1)}, bf16[64,1152]{1,0:T(8,128)(2,1)S(1)}, u32[]{:S(2)}, u32[]{:S(2)}) collective-permute-start(bf16[64,1152]{1,0:T(8,128)(2,1)S(1)} %get-tuple-element.17), channel_id=1, source_target_pairs={{0,8},{8,0},{16,24},{24,16},{32,40},{40,32},{48,56},{56,48},{64,72... | collective-permute-start | bytes 442376 | tf_op jit(solution)/shard_map/ppermute | solution.py:219
  11.1 10.5 %all_to_all.20.w_ref = bf16[8,8,512]{2,1,0:T(8,128)(2,1)S(1)} all-to-all(bf16[8,8,512]{2,1,0:T(8,128)(2,1)S(1)} %get-tuple-element.18), channel_id=1, replica_groups={{7,0,6,1,5,2,4,3},{15,8,14,9,13,10,12,11},{23,16,22,17,21,18,20,19},{31..., dimensions={0} | all-to-all | bytes 131072 | tf_op jit(solution)/shard_map/all_to_all | solution.py:206
  21.6 0.0 collective-permute-done.other_ref
  21.6 0.3 pack.1
  21.8 0.2 reshape.12
  22.1 21.8 %all_to_all.21 = bf16[32,2,4224]{2,1,0:T(2,128)(2,1)S(1)} all-to-all(bf16[32,2,4224]{2,1,0:T(2,128)(2,1)S(1)} %reshape.12), channel_id=1, replica_groups={{496,480,464,448,432,416,400,384,368,352,336,320,304,288,272,256,240,22..., dimensions={0} | all-to-all | bytes 1081344 | tf_op jit(solution)/shard_map/all_to_all | solution.py:227
  43.9 0.2 reshape.13.refs_0_
  44.1 1.3 %own_rows.1 = bf16[8,64,1024]{2,1,0:T(8,128)(2,1)} custom-call(bf16[64,4224]{1,0:T(8,128)(2,1)S(1)} %reshape.13.refs_0_), custom_call_target="tpu_custom_call" | custom-call | flops 20000000 | bytes 1500000 | tf_op jit(solution)/shard_map/own_rows/pallas_call | solution.py:231
  45.4 5.9 %all-to-all-start.2 = ((bf16[8,64,1024]{2,1,0:T(8,128)(2,1)}), bf16[8,64,1024]{2,1,0:T(8,128)(2,1)S(1)}, u32[]{:S(2)}, u32[]{:S(2)}) async-start(bf16[8,64,1024]{2,1,0:T(8,128)(2,1)} %own_rows.1), calls=%async_computation.2 | async-start | bytes 2097152 | tf_op jit(solution)/shard_map/all_to_all | solution.py:238
  51.3 3.1 %collective-permute-start.1 = (bf16[64,2048]{1,0:T(8,128)(2,1)S(1)}, bf16[64,2048]{1,0:T(8,128)(2,1)S(1)}, u32[]{:S(2)}, u32[]{:S(2)}) collective-permute-start(bf16[64,2048]{1,0:T(8,128)(2,1)S(1)} %slice.4), channel_id=1, source_target_pairs={{0,1},{1,0},{2,3},{3,2},{4,5},{5,4},{6,7},{7,6},{8,9},{9,8},{10,11... | collective-permute-start | bytes 786440 | tf_op jit(solution)/shard_map/ppermute | solution.py:241
  54.4 4.6 %collective-permute-done.1 = bf16[64,2048]{1,0:T(8,128)(2,1)S(1)} collective-permute-done((bf16[64,2048]{1,0:T(8,128)(2,1)S(1)}, bf16[64,2048]{1,0:T(8,128)(2,1)S(1)}, u32[]{:S(2)}, u32[]{:S(2)}) %collective-permute-start.1) | collective-permute-done | bytes 262176 | tf_op jit(solution)/shard_map/ppermute | solution.py:241
  59.1 4.8 %collective-permute-start.2 = (bf16[128,2048]{1,0:T(8,128)(2,1)S(1)}, bf16[128,2048]{1,0:T(8,128)(2,1)S(1)}, u32[]{:S(2)}, u32[]{:S(2)}) collective-permute-start(bf16[128,2048]{1,0:T(8,128)(2,1)S(1)} %pad_maximum_fusion.mine_ref), channel_id=1, source_target_pairs={{0,8},{8,0},{16,24},{24,16},{32,40},{40,32},{48,56},{56,48},{64,72... | collective-permute-start | bytes 1572872 | tf_op jit(solution)/shard_map/ppermute | solution.py:243
  63.9 1.5 %collective-permute-done.2.theirs_ref = bf16[128,2048]{1,0:T(8,128)(2,1)S(1)} collective-permute-done((bf16[128,2048]{1,0:T(8,128)(2,1)S(1)}, bf16[128,2048]{1,0:T(8,128)(2,1)S(1)}, u32[]{:S(2)}, u32[]{:S(2)}) %collective-permute-start.2) | collective-permute-done | bytes 524320 | tf_op jit(solution)/shard_map/ppermute | solution.py:243
  65.4 0.0 all-to-all-done.2
  65.4 0.8 project.1
  66.2 13.8 %all_to_all.22.back_ref = bf16[8,64,512]{2,1,0:T(8,128)(2,1)S(1)} all-to-all(bf16[8,64,512]{2,1,0:T(8,128)(2,1)S(1)} %bitcast.6), channel_id=1, replica_groups={{0,16,32,48,64,80,96,112},{8,24,40,56,72,88,104,120},{128,144,160,176,1..., dimensions={0} | all-to-all | bytes 1048576 | tf_op jit(solution)/shard_map/all_to_all | solution.py:253
  80.0 0.8 %lay_out.1 = bf16[64,4096]{1,0:T(8,128)(2,1)} custom-call(bf16[8,64,512]{2,1,0:T(8,128)(2,1)S(1)} %all_to_all.22.back_ref), custom_call_target="tpu_custom_call" | custom-call | tf_op jit(solution)/shard_map/lay_out/pallas_call | solution.py:256
  (2 shorter events, 0.1 us)
Async XLA Ops:
  2.3 19.3 %collective-permute-start = (bf16[64,1152]{1,0:T(8,128)(2,1)S(1)}, bf16[64,1152]{1,0:T(8,128)(2,1)S(1)}, u32[]{:S(2)}, u32[]{:S(2)}) collective-permute-start(bf16[64,1152]{1,0:T(8,128)(2,1)S(1)} %get-tuple-element.17), channel_id=1, source_target_pairs={{0,8},{8,0},{16,24},{24,16},{32,40},{40,32},{48,56},{56,48},{64,72... | collective-permute-start | bytes 442376 | tf_op jit(solution)/shard_map/ppermute | solution.py:219
  45.4 20.0 %all-to-all-start.2 = ((bf16[8,64,1024]{2,1,0:T(8,128)(2,1)}), bf16[8,64,1024]{2,1,0:T(8,128)(2,1)S(1)}, u32[]{:S(2)}, u32[]{:S(2)}) async-start(bf16[8,64,1024]{2,1,0:T(8,128)(2,1)} %own_rows.1), calls=%async_computation.2 | async-start | bytes 2097152 | tf_op jit(solution)/shard_map/all_to_all | solution.py:238
  51.3 7.7 %collective-permute-start.1 = (bf16[64,2048]{1,0:T(8,128)(2,1)S(1)}, bf16[64,2048]{1,0:T(8,128)(2,1)S(1)}, u32[]{:S(2)}, u32[]{:S(2)}) collective-permute-start(bf16[64,2048]{1,0:T(8,128)(2,1)S(1)} %slice.4), channel_id=1, source_target_pairs={{0,1},{1,0},{2,3},{3,2},{4,5},{5,4},{6,7},{7,6},{8,9},{9,8},{10,11... | collective-permute-start | bytes 786440 | tf_op jit(solution)/shard_map/ppermute | solution.py:241
  59.1 6.3 %collective-permute-start.2 = (bf16[128,2048]{1,0:T(8,128)(2,1)S(1)}, bf16[128,2048]{1,0:T(8,128)(2,1)S(1)}, u32[]{:S(2)}, u32[]{:S(2)}) collective-permute-start(bf16[128,2048]{1,0:T(8,128)(2,1)S(1)} %pad_maximum_fusion.mine_ref), channel_id=1, source_target_pairs={{0,8},{8,0},{16,24},{24,16},{32,40},{40,32},{48,56},{56,48},{64,72... | collective-permute-start | bytes 1572872 | tf_op jit(solution)/shard_map/ppermute | solution.py:243
